TPU v7x, 32 devices: a whole 2x2x4 slice. The times are simulated.
32 devices in a mesh: rep: 8 (over z, y), shard: 4 (over x, core).
Axes of the slice: x: 2, y: 2, z: 4, core: 2. Of those that a mesh axis runs over, the one named last changes fastest.
Arguments:
- hidden_in: bfloat16 [32768, 1024], P(('rep', 'shard')), may hold values from -6 to 6
- teacher: bfloat16 [32768, 1024], P(('rep', 'shard')), may hold values from -6 to 6
- cotangent: bfloat16 [32768, 1024], P(('rep', 'shard')), may hold values from -6 to 6
- lengths: int32 [32], P(('rep', 'shard')), may hold values from 512 to 1024, as said below
- norm_attn: float32 [1024], replicated, may hold values from 0.5 to 1.5
- w_in: bfloat16 [1024, 6144], P('shard'), may hold values from -0.1875 to 0.1875
- w_small: bfloat16 [1024, 24], P('shard'), may hold values from -0.1875 to 0.1875
- conv_w: float32 [4, 5120], replicated, may hold values from -3 to 3
- a_log: float32 [8], replicated, may hold values from -6 to 0.5
- dt_bias: float32 [8], replicated, may hold values from -2 to 1
- norm_head: float32 [128], replicated, may hold values from 0.5 to 1.5
- w_out: bfloat16 [1024, 1024], P('shard'), may hold values from -0.1875 to 0.1875
- norm_mlp: float32 [1024], replicated, may hold values from 0.5 to 1.5
- w_mlp_in: bfloat16 [1024, 5632], P('shard'), may hold values from -0.1875 to 0.1875
- w_mlp_down: bfloat16 [2816, 1024], P('shard'), may hold values from -0.109375 to 0.109375
Outputs:
- layer_out: bfloat16 [32768, 1024], P(('rep', 'shard'))
- loss: float32 [], replicated
- grad_hidden: bfloat16 [32768, 1024], P(('rep', 'shard'))
- grad_norm_attn: float32 [1024], replicated
- grad_w_in: float32 [1024, 6144], P('shard')
- grad_w_small: float32 [1024, 24], P('shard')
- grad_conv_w: float32 [4, 5120], replicated
- grad_a_log: float32 [8], replicated
- grad_dt_bias: float32 [8], replicated
- grad_norm_head: float32 [128], replicated
- grad_w_out: float32 [1024, 1024], P('shard')
- grad_norm_mlp: float32 [1024], replicated
- grad_w_mlp_in: float32 [1024, 5632], P('shard')
- grad_w_mlp_down: float32 [2816, 1024], P('shard')
Inputs may be any that keep to these rules, and one draw needn't show every extreme that they name: `lengths`: each sequence's valid slots are a prefix of its 1024 slots; in every draw some sequence is full and some holds 512 valid slots.
All inputs are finite; a program needn't handle non-finite values.
Results may differ from a plain program's by a relative error of at most 0.014.
Values may be sent and summed in bfloat16 or wider, within the bound.
No kernel may reach another device: no remote copies, remote signals or barrier semaphores. Data moves between devices by JAX's collectives and lax.ppermute only.
A program may use at most 512 MiB of HBM per device.

v0:
```python
import jax
import jax.numpy as jnp
from jax import lax
from jax.sharding import PartitionSpec as P

HEADS = 8
DK = 128
DV = 128
HOUSE = 2
BLOCK = 64


EPSILON = 1e-06
PRECISE = lax.Precision.HIGHEST


def norm_rows(row_values, gain_row):
    return (
        row_values
        * lax.rsqrt(jnp.mean(row_values * row_values, axis=-1, keepdims=True) + EPSILON)
        * gain_row
    )


def dot_plain(operand_a, operand_b):
    return jnp.dot(operand_a, operand_b, preferred_element_type=jnp.float32)


def dot_right_t(operand_a, operand_b):
    return lax.dot_general(
        operand_a, operand_b, (((1,), (1,)), ((), ())), preferred_element_type=jnp.float32
    )


def dot_left_t(operand_a, operand_b):
    return lax.dot_general(
        operand_a, operand_b, (((0,), (0,)), ((), ())), preferred_element_type=jnp.float32
    )


def block_coupling(keys_in, beta_rows, log_gates):
    row_count = keys_in.shape[0]
    cumulated = jnp.cumsum(log_gates, axis=0).T
    keys_head = jnp.transpose(keys_in, (1, 0, 2))
    betas_head = beta_rows.T
    row_index = lax.broadcasted_iota(jnp.int32, (row_count, row_count), 0)
    col_index = lax.broadcasted_iota(jnp.int32, (row_count, row_count), 1)
    strictly = (col_index < row_index)[None]
    spread_log = cumulated[:, :, None] - cumulated[:, None, :]
    fading = jnp.where(strictly, jnp.exp(jnp.where(strictly, spread_log, 0.0)), 0.0)
    intersections = jnp.einsum("hrc,hic->hri", keys_head, keys_head, precision=PRECISE)
    return intersections * fading * betas_head[:, None, :]


def block_step(memory, pieces):
    queries, keys_in, values_in, beta_rows, log_gates, inverse = pieces
    row_count = keys_in.shape[0]
    query_count = queries.shape[0]
    substeps = row_count // query_count
    cumulated = jnp.cumsum(log_gates, axis=0).T
    keys_head = jnp.transpose(keys_in, (1, 0, 2))
    values_head = jnp.transpose(values_in, (1, 0, 2))
    queries_head = jnp.transpose(queries, (1, 0, 2))
    betas_head = beta_rows.T
    carried = jnp.einsum("hrc,hcd->hrd", keys_head, memory, precision=PRECISE)
    targets = values_head - jnp.exp(cumulated)[:, :, None] * carried
    updates = jnp.einsum("hri,hid->hrd", inverse, targets, precision=PRECISE)
    read_row = (
        lax.broadcasted_iota(jnp.int32, (query_count, row_count), 0) * substeps + substeps - 1
    )
    read_col = lax.broadcasted_iota(jnp.int32, (query_count, row_count), 1)
    visible = (read_col <= read_row)[None]
    read_log = cumulated[:, substeps - 1 :: substeps]
    query_spread = read_log[:, :, None] - cumulated[:, None, :]
    query_fading = jnp.where(visible, jnp.exp(jnp.where(visible, query_spread, 0.0)), 0.0)
    scores = (
        jnp.einsum("htc,hic->hti", queries_head, keys_head, precision=PRECISE)
        * query_fading
        * betas_head[:, None, :]
    )
    outputs = jnp.exp(read_log)[:, :, None] * jnp.einsum(
        "htc,hcd->htd", queries_head, memory, precision=PRECISE
    )
    outputs = outputs + jnp.einsum("hti,hid->htd", scores, updates, precision=PRECISE)
    last_log = cumulated[:, -1]
    carry_weights = jnp.exp(last_log[:, None] - cumulated) * betas_head
    new_memory = jnp.exp(last_log)[:, None, None] * memory + jnp.einsum(
        "hic,hid->hcd", keys_head * carry_weights[:, :, None], updates, precision=PRECISE
    )
    return (new_memory, jnp.transpose(outputs, (1, 0, 2)))


def sequence_mix(queries, keys_in, values_in, beta_rows, log_gates):
    block_count = queries.shape[0] // BLOCK
    memory = jnp.zeros((HEADS, DK, DV), jnp.float32)
    keys_blocks = keys_in.reshape(block_count, BLOCK * HOUSE, HEADS, DK)
    beta_blocks = beta_rows.reshape(block_count, BLOCK * HOUSE, HEADS)
    gate_blocks = log_gates.reshape(block_count, BLOCK * HOUSE, HEADS)
    coupling = jax.vmap(block_coupling)(keys_blocks, beta_blocks, gate_blocks)
    identity = jnp.broadcast_to(jnp.eye(BLOCK * HOUSE, dtype=jnp.float32), coupling.shape)
    inverse = lax.linalg.triangular_solve(
        coupling, identity, left_side=True, lower=True, unit_diagonal=True
    )
    pieces = (
        queries.reshape(block_count, BLOCK, HEADS, DK),
        keys_blocks,
        values_in.reshape(block_count, BLOCK * HOUSE, HEADS, DV),
        beta_blocks,
        gate_blocks,
        inverse,
    )
    final_memory, outputs = lax.scan(jax.checkpoint(block_step), memory, pieces)
    return outputs.reshape(queries.shape[0], HEADS, DV)


def mixer_core(proj_rows, small_rows, conv_w, a_log, dt_bias, norm_head):
    slot_count = proj_rows.shape[0]
    tap_count = conv_w.shape[0]
    channel_count = conv_w.shape[1]
    conv_input = proj_rows[:, :channel_count]
    padded = jnp.concatenate(
        [jnp.zeros((tap_count - 1, channel_count), jnp.float32), conv_input], axis=0
    )
    conv_out = conv_w[0] * padded[0:slot_count]
    for offset in range(1, tap_count):
        conv_out = conv_out + conv_w[offset] * padded[offset : offset + slot_count]
    active = jax.nn.silu(conv_out)
    query_width = HEADS * DK
    key_width = HOUSE * HEADS * DK
    queries = active[:, :query_width].reshape(slot_count, HEADS, DK)
    keys_in = active[:, query_width : query_width + key_width].reshape(
        slot_count * HOUSE, HEADS, DK
    )
    values_in = active[:, query_width + key_width :].reshape(slot_count * HOUSE, HEADS, DV)
    queries = (
        queries
        * lax.rsqrt(jnp.sum(queries * queries, axis=-1, keepdims=True) + EPSILON)
        * DK ** (-0.5)
    )
    keys_in = keys_in * lax.rsqrt(jnp.sum(keys_in * keys_in, axis=-1, keepdims=True) + EPSILON)
    beta_rows = jax.nn.sigmoid(small_rows[:, : HOUSE * HEADS]).reshape(slot_count * HOUSE, HEADS)
    decays = -jnp.exp(a_log) * jax.nn.softplus(small_rows[:, HOUSE * HEADS :] + dt_bias)
    log_gates = jnp.concatenate(
        [decays[:, None, :], jnp.zeros((slot_count, HOUSE - 1, HEADS), jnp.float32)], axis=1
    ).reshape(slot_count * HOUSE, HEADS)
    mixed_heads = sequence_mix(queries, keys_in, values_in, beta_rows, log_gates)
    mixed_heads = (
        mixed_heads
        * lax.rsqrt(jnp.mean(mixed_heads * mixed_heads, axis=-1, keepdims=True) + EPSILON)
        * norm_head
    )
    out_gate = proj_rows[:, channel_count:].reshape(slot_count, HEADS, DV)
    return (mixed_heads * jax.nn.silu(out_gate)).reshape(slot_count, HEADS * DV)


def shards(
    hidden_in,
    teacher,
    cotangent,
    lengths,
    norm_attn,
    w_in,
    w_small,
    conv_w,
    a_log,
    dt_bias,
    norm_head,
    w_out,
    norm_mlp,
    w_mlp_in,
    w_mlp_down,
):
    row_count = hidden_in.shape[0]
    seq_here = lengths.shape[0]
    slot_count = row_count // seq_here
    own_rows = w_small.shape[0]
    w_in_all, w_small_all, w_out_all = (
        lax.all_gather(w_in, "shard", axis=0, tiled=True),
        lax.all_gather(w_small, "shard", axis=0, tiled=True),
        lax.all_gather(w_out, "shard", axis=0, tiled=True),
    )
    hidden32 = hidden_in.astype(jnp.float32)
    normed_in, norm_in_pull = jax.vjp(norm_rows, hidden32, norm_attn)
    normed_low = normed_in.astype(jnp.bfloat16)
    proj_rows = dot_plain(normed_low, w_in_all)
    small_rows = dot_plain(normed_low, w_small_all)

    def mixer_all(proj_part, small_part, conv_part, log_part, bias_part, gain_part):
        per_seq = jax.vmap(mixer_core, in_axes=(0, 0, None, None, None, None))(
            proj_part.reshape(seq_here, slot_count, proj_part.shape[1]),
            small_part.reshape(seq_here, slot_count, small_part.shape[1]),
            conv_part,
            log_part,
            bias_part,
            gain_part,
        )
        return per_seq.reshape(row_count, per_seq.shape[2])

    mixed_rows, mixer_pull = jax.vjp(
        mixer_all, proj_rows, small_rows, conv_w, a_log, dt_bias, norm_head
    )
    mixed_low = mixed_rows.astype(jnp.bfloat16)
    residual = hidden32 + dot_plain(mixed_low, w_out_all)
    w_mlp_in_all, w_down_all = (
        lax.all_gather(w_mlp_in, "shard", axis=0, tiled=True),
        lax.all_gather(w_mlp_down, "shard", axis=0, tiled=True),
    )
    normed_mid, norm_mid_pull = jax.vjp(norm_rows, residual, norm_mlp)
    mid_low = normed_mid.astype(jnp.bfloat16)
    gate_up = dot_plain(mid_low, w_mlp_in_all)
    unit_count = w_down_all.shape[0]
    gate_part = gate_up[:, :unit_count]
    up_part = gate_up[:, unit_count:]
    sigmoid_gate = jax.nn.sigmoid(gate_part)
    silu_gate = gate_part * sigmoid_gate
    product_low = (silu_gate * up_part).astype(jnp.bfloat16)
    output32 = residual + dot_plain(product_low, w_down_all)
    slot_index = lax.broadcasted_iota(jnp.int32, (seq_here, slot_count), 1)
    valid_rows = (slot_index < lengths[:, None]).astype(jnp.float32).reshape(row_count, 1)
    deviation = output32 - teacher.astype(jnp.float32)
    loss_sum, valid_count = lax.psum(
        (jnp.sum(valid_rows * deviation * deviation), jnp.sum(lengths).astype(jnp.float32)),
        ("rep", "shard"),
    )
    loss_value = loss_sum / (valid_count * output32.shape[1])
    grad_out = valid_rows * (cotangent.astype(jnp.float32) + deviation)
    grad_out_low = grad_out.astype(jnp.bfloat16)
    w_mlp_in_back, w_down_back = (
        lax.all_gather(w_mlp_in, "shard", axis=0, tiled=True),
        lax.all_gather(w_mlp_down, "shard", axis=0, tiled=True),
    )
    grad_product = dot_right_t(grad_out_low, w_down_back)
    grad_w_down = dot_left_t(product_low, grad_out_low)
    grad_gate = grad_product * up_part * sigmoid_gate * (1.0 + gate_part * (1.0 - sigmoid_gate))
    grad_up = grad_product * silu_gate
    grad_gate_up = jnp.concatenate([grad_gate, grad_up], axis=1).astype(jnp.bfloat16)
    grad_mid = dot_right_t(grad_gate_up, w_mlp_in_back)
    grad_w_mlp_in = dot_left_t(mid_low, grad_gate_up)
    grad_res_part, grad_norm_mlp = norm_mid_pull(grad_mid)
    grad_residual = grad_out + grad_res_part
    own_mlp_in, own_down = (
        lax.psum_scatter(
            grad_w_mlp_in.astype(jnp.bfloat16), "shard", scatter_dimension=0, tiled=True
        ).astype(jnp.float32),
        lax.psum_scatter(
            grad_w_down.astype(jnp.bfloat16), "shard", scatter_dimension=0, tiled=True
        ).astype(jnp.float32),
    )
    grad_res_low = grad_residual.astype(jnp.bfloat16)
    w_in_back, w_small_back, w_out_back = (
        lax.all_gather(w_in, "shard", axis=0, tiled=True),
        lax.all_gather(w_small, "shard", axis=0, tiled=True),
        lax.all_gather(w_out, "shard", axis=0, tiled=True),
    )
    grad_mixed = dot_right_t(grad_res_low, w_out_back)
    grad_w_out = dot_left_t(mixed_low, grad_res_low)
    grad_proj, grad_small, grad_conv, grad_log, grad_bias, grad_gain = mixer_pull(grad_mixed)
    grad_proj_low = grad_proj.astype(jnp.bfloat16)
    grad_small_low = grad_small.astype(jnp.bfloat16)
    grad_normed = dot_right_t(grad_proj_low, w_in_back) + dot_right_t(grad_small_low, w_small_back)
    grad_w_in = dot_left_t(normed_low, grad_proj_low)
    grad_w_small = dot_left_t(normed_low, grad_small_low)
    grad_in_part, grad_norm_attn = norm_in_pull(grad_normed)
    grad_hidden = (grad_residual + grad_in_part).astype(jnp.bfloat16)
    sum_norm_attn, sum_conv, sum_log, sum_bias, sum_gain, sum_norm_mlp, sum_small = lax.psum(
        (grad_norm_attn, grad_conv, grad_log, grad_bias, grad_gain, grad_norm_mlp, grad_w_small),
        ("rep", "shard"),
    )
    own_small = lax.dynamic_slice_in_dim(sum_small, lax.axis_index("shard") * own_rows, own_rows, 0)
    own_in, own_out = (
        lax.psum_scatter(
            grad_w_in.astype(jnp.bfloat16), "shard", scatter_dimension=0, tiled=True
        ).astype(jnp.float32),
        lax.psum_scatter(
            grad_w_out.astype(jnp.bfloat16), "shard", scatter_dimension=0, tiled=True
        ).astype(jnp.float32),
    )
    own_in, own_out, own_mlp_in, own_down = (
        lax.psum(own_in.astype(jnp.bfloat16), "rep").astype(jnp.float32),
        lax.psum(own_out.astype(jnp.bfloat16), "rep").astype(jnp.float32),
        lax.psum(own_mlp_in.astype(jnp.bfloat16), "rep").astype(jnp.float32),
        lax.psum(own_down.astype(jnp.bfloat16), "rep").astype(jnp.float32),
    )
    return (
        output32.astype(jnp.bfloat16),
        loss_value,
        grad_hidden,
        sum_norm_attn,
        own_in,
        own_small,
        sum_conv,
        sum_log,
        sum_bias,
        sum_gain,
        own_out,
        sum_norm_mlp,
        own_mlp_in,
        own_down,
    )


def solution(mesh):
    in_specs = (
        P(("rep", "shard"), None),
        P(("rep", "shard"), None),
        P(("rep", "shard"), None),
        P(("rep", "shard")),
        P(),
        P("shard", None),
        P("shard", None),
        P(),
        P(),
        P(),
        P(),
        P("shard", None),
        P(),
        P("shard", None),
        P("shard", None),
    )
    out_specs = (
        P(("rep", "shard"), None),
        P(),
        P(("rep", "shard"), None),
        P(),
        P("shard", None),
        P("shard", None),
        P(),
        P(),
        P(),
        P(),
        P("shard", None),
        P(),
        P("shard", None),
        P("shard", None),
    )
    return jax.shard_map(shards, mesh=mesh, in_specs=in_specs, out_specs=out_specs, check_vma=False)
```

profile of v0, /device:TPU:0, one launch (start us, length us, event | category | flops | bytes accessed | tf_op | source)
XLA Modules:
  0.0 4014.8 jit_solution(10543486210761847069)
XLA Ops:
  13.5 6.2 all_gather.20
  42.4 52.0 %all-gather.5.cloned.1.call-done = bf16[1024,6144]{1,0:T(8,128)(2,1)} async-done(((bf16[256,6144]{1,0:T(8,128)(2,1)}), bf16[1024,6144]{1,0:T(8,128)(2,1)}) %all-gather.5.cloned.1.call-update) | async-done | bytes 12582928 | tf_op jit(solution)/shard_map/all_gather | solution.py:178
  94.4 21.1 convolution_bitcast_fusion.8
  115.5 16.8 slice.113
  132.4 45.0 %fusion.127 = (f32[1,1024,5120]{2,1,0:T(8,128)}, f32[1,1024,5120]{2,1,0:T(8,128)}) fusion(f32[1,1024,5120]{2,1,0:T(8,128)} %slice.113, f32[5120]{0:T(1024)S(1)} %bitcast.855, f32[5120]{0:T(1024)S(1)} %bitcast.857, f32[5120]{0:T(1024)S(1)} %bitcast.853, f32[5120]{0:T(1024)S(1)} %bitcast.851), kind=kLoop, calls=%fused_computation.197 | loop fusion | flops 57671680 | bytes 62996480 | tf_op jit(solution)/shard_map/jvp(vmap(jit(silu)))/mul | solution.py:127
  177.4 11.0 fusion.234
  188.4 9.2 reshape.1394
  197.7 9.4 reshape.1395
  207.1 9.5 reshape.1397
  216.6 5.1 slice_bitcast_fusion.2
  229.4 9.4 copy_multiply_fusion.1
  238.9 21.6 fusion.134
  263.7 5.2 add_bitcast_fusion
  268.9 1259.0 %custom-call.5 = f32[1,16,8,1,128,128]{4,5,3,2,1,0:T(8,128)} custom-call(f32[1,16,8,1,128,128]{5,4,3,2,1,0:T(8,128)} %add_bitcast_fusion), custom_call_target="InvertDiagBlocksLowerTriangular" | custom-call | tf_op jit(solution)/shard_map/jvp(vmap())/triangular_solve | solution.py:101
  1527.8 9.8 reshape.1402
  1550.8 16.6 fusion.140
  1571.7 316.9 %while.47 = (s32[]{:T(128)}, f32[1,8,128,128]{3,2,1,0:T(8,128)S(1)}, f32[16,1,64,8,128]{4,2,3,1,0:T(8,128)}, f32[16,1,8,128,128]{4,3,2,1,0:T(8,128)}, f32[16,1,1...) while((s32[]{:T(128)}, ...), condition=%wide.region_6.7_spmd.clone.clone, body=%wide.region_4.6_spmd.clone.clone.sunk | while | flops 907740160 | bytes 11392390 | solution.py:112
  1888.6 7.7 copy.320
  1900.8 5.6 fusion.179
  1906.5 6.8 multiply_reduce_fusion.13
  1913.3 21.1 fusion.224
  1934.4 12.2 multiply_convert_fusion.2
  1946.6 13.7 fusion.190
  1960.3 20.2 multiply_convert_fusion.1
  1980.5 21.4 multiply_reduce_fusion.9
  2002.0 10.3 fusion.153
  2018.0 4.7 fusion.194
  2022.8 6.6 fusion.155
  2035.5 7.9 multiply_reduce_fusion.10
  2044.5 4.9 add_add_fusion.3
  2049.5 8.0 convolution_convert_fusion.2
  2074.6 1061.4 %while.46 = (s32[]{:T(128)}, f32[1,8,128,128]{2,3,1,0:T(8,128)}, f32[16,1,64,8,128]{4,3,2,0,1:T(8,128)}, f32[16,1,128,8,128]{4,2,3,0,1:T(8,128)}, f32[16,1,128,8...) while((s32[]{:T(128)}, f32[1,8,128,128]{2,3,1,0:T(8,128)}, ...), condition=%wide.region_25.26_spmd.clone, body=%wide.region_14.25_spmd.clone.sunk | while | flops 2421509120 | bytes 52434800 | solution.py:112
  3136.0 4.9 broadcast_multiply_fusion.4
  3142.2 21.0 fusion.136
  3163.1 19.9 convolution_convert_fusion.1
  3183.1 4.6 fusion.162
  3187.8 5.1 transpose.299
  3196.5 5.5 broadcast_in_dim.293
  3204.8 4.9 mul.1293
  3209.7 22.6 fusion.226
  3232.4 16.9 fusion.130
  3249.3 22.4 bitcast_add_fusion.4
  3271.7 9.9 copy.340
  3281.6 9.2 reshape.1409
  3290.8 7.6 multiply_reduce_fusion.7
  3299.1 6.3 broadcast_in_dim.290
  3305.5 9.3 broadcast_in_dim.291
  3315.1 6.3 mul.1282
  3321.5 9.3 mul.1283
  3330.7 9.5 transpose.296
  3340.2 8.4 add_add_fusion.2
  3348.6 13.1 add_add_fusion
  3361.8 44.9 %multiply_reduce_fusion.4 = (f32[5120]{0:T(1024)S(1)}, f32[5120]{0:T(1024)S(1)}, f32[5120]{0:T(1024)S(1)}, f32[5120]{0:T(1024)S(1)}, f32[1,1024,5120]{2,1,0:T(8,128)}) fusion(f32[1,1024,5120]{2,1,0:T(8,128)} %slice.113, f32[1,1024,6144]{2,1,0:T(8,128)} %convolution_bitcast_fusion.8, f32[1,1024,5120]{2,1,0:T(8,128)} %get-tuple-element.897, ...), kind=kLoop, calls=%fused_computation.194 | loop fusion | flops 99594240 | bytes 104939520 | tf_op jit(solution)/shard_map/transpose(jvp(vmap()))/reduce_sum | solution.py:126
  3406.7 34.0 broadcast_multiply_fusion
  3440.7 36.1 pad_add_fusion
  3476.9 19.9 convolution_convert_fusion
  3503.4 23.3 fusion.236
  3531.6 65.4 %reduce-scatter.5.cloned.1.call-done = bf16[256,6144]{1,0:T(8,128)(2,1)} async-done(((bf16[1024,6144]{1,0:T(8,128)(2,1)}), bf16[256,6144]{1,0:T(8,128)(2,1)}) %reduce-scatter.5.cloned.1.call-update) | async-done | bytes 3145744 | tf_op jit(solution)/shard_map/reduce_scatter | solution.py:271
  3599.9 22.3 fusion.151
  3622.2 40.0 all-reduce.19
  3666.2 5.8 fusion.157
  3677.2 49.2 %all-reduce.25.cloned.1.call-done = (f32[1024,24]{0,1:T(8,128)}, f32[4,5120]{1,0:T(4,128)}) async-done(((f32[1024,24]{0,1:T(8,128)}, f32[4,5120]{1,0:T(4,128)}), (f32[1024,24]{0,1:T(8,128)}, f32[4,5120]{1,0:T(4,128)})) %all-reduce.25.cloned.1.call-update) | async-done | bytes 180240 | tf_op jit(solution)/shard_map/psum | solution.py:265
  3727.8 266.4 %all-reduce.27.cloned.1.call-done = (bf16[256,6144]{1,0:T(8,128)(2,1)}, bf16[256,1024]{1,0:T(8,128)(2,1)}, bf16[256,5632]{1,0:T(8,128)(2,1)}, bf16[704,1024]{1,0:T(8,128)(2,1)}) async-done(((bf16[256,6144]{1,0:T(8,128)(2,1)}, bf16[256,1024]{1,0:T(8,128)(2,1)}, bf16[256,5632]{1,0:T(8,128)(2,1)}, bf16[704,1024]{1,0:T(8,128)(2,1)}), (bf16[256,6144]{1,0:T(8,128)(2,1)}, bf16[256,1024]{1,0:T(8,128)(2,1)}, ...) | async-done | bytes 7995408 | tf_op jit(solution)/shard_map/psum | solution.py:279
  3994.3 5.5 convert_element_type.112
  (2086 shorter events, 1502.2 us)
Async XLA Ops:
  7.2 87.2 %all-gather.5.cloned.1.call-start = ((), (), s32[]{:S(2)}) async-start(), calls=%async_computation.4 | async-start | bytes 15728640 | tf_op jit(solution)/shard_map/all_gather | solution.py:178
  7.9 1898.5 %all-gather.7.cloned.1.call-start = ((), (), s32[]{:S(2)}) async-start(), calls=%async_computation.5 | async-start | bytes 2621440 | tf_op jit(solution)/shard_map/all_gather | solution.py:180
  8.7 1904.6 %all-gather.9.cloned.1.call-start = ((), (), s32[]{:S(2)}) async-start(), calls=%async_computation.6 | async-start | bytes 14417920 | tf_op jit(solution)/shard_map/all_gather | solution.py:205
  9.4 1937.2 %all-gather.11.cloned.1.call-start = ((), (), s32[]{:S(2)}) async-start(), calls=%async_computation.7 | async-start | bytes 7208960 | tf_op jit(solution)/shard_map/all_gather | solution.py:206
  10.0 3521.6 %reduce-scatter.7.cloned.1.call-start = ((), (), s32[]{:S(2)}) async-start(), calls=%async_computation.9 | async-start | bytes 2621440 | tf_op jit(solution)/shard_map/reduce_scatter | solution.py:274
  12.9 1893.5 %copy-start.17 = (bf16[1024,1024]{0,1:T(8,128)(2,1)}, bf16[1024,1024]{0,1:T(8,128)(2,1)S(1)}, u32[]{:S(2)}) copy-start(bf16[1024,1024]{0,1:T(8,128)(2,1)S(1)} %copy.300) | copy-start | bytes 6291460
  13.5 80.9 %copy-start.74 = (f32[1024]{0:T(1024)}, f32[1024]{0:T(1024)S(1)}, u32[]{:S(2)}) copy-start(f32[1024]{0:T(1024)S(1)} %fusion.214) | copy-start | bytes 12292
  20.3 16.8 copy-start.47
  26.2 106.2 %copy-start.59 = (f32[1,5120]{1,0:T(1,128)}, f32[1,5120]{1,0:T(1,128)S(1)}, u32[]{:S(2)}) copy-start(f32[1,5120]{1,0:T(1,128)S(1)} %get-tuple-element.929) | copy-start | bytes 61444
  26.2 106.2 %copy-start.61 = (f32[1,5120]{1,0:T(1,128)}, f32[1,5120]{1,0:T(1,128)S(1)}, u32[]{:S(2)}) copy-start(f32[1,5120]{1,0:T(1,128)S(1)} %get-tuple-element.930) | copy-start | bytes 61444
  26.2 106.2 %copy-start.63 = (f32[1,5120]{1,0:T(1,128)}, f32[1,5120]{1,0:T(1,128)S(1)}, u32[]{:S(2)}) copy-start(f32[1,5120]{1,0:T(1,128)S(1)} %get-tuple-element.931) | copy-start | bytes 61444
  27.9 232.6 %copy-start.37 = (f32[16,8,128]{2,1,0:T(8,128)}, f32[16,8,128]{2,1,0:T(8,128)S(1)}, u32[]{:S(2)}) copy-start(f32[16,8,128]{2,1,0:T(8,128)S(1)} %copy.311) | copy-start | bytes 196612
  32.4 228.1 %copy-start.26 = (f32[16,8,128]{2,1,0:T(8,128)}, f32[16,8,128]{2,1,0:T(8,128)S(1)}, u32[]{:S(2)}) copy-start(f32[16,8,128]{2,1,0:T(8,128)S(1)} %copy.308) | copy-start | bytes 196612
  32.5 228.0 %copy-start.53 = (pred[128,128]{1,0:T(8,128)(4,1)}, pred[128,128]{1,0:T(8,128)(4,1)S(1)}, u32[]{:S(2)}) copy-start(pred[128,128]{1,0:T(8,128)(4,1)S(1)} %get-tuple-element.944) | copy-start | bytes 49156
  32.5 228.0 %copy-start.55 = (pred[128,128]{1,0:T(8,128)(4,1)}, pred[128,128]{1,0:T(8,128)(4,1)S(1)}, u32[]{:S(2)}) copy-start(pred[128,128]{1,0:T(8,128)(4,1)S(1)} %get-tuple-element.945) | copy-start | bytes 49156
  115.5 16.9 copy-start.65
  1913.3 88.7 %copy-start.77 = (f32[1024]{0:T(1024)}, f32[1024]{0:T(1024)S(1)}, u32[]{:S(2)}) copy-start(f32[1024]{0:T(1024)S(1)} %fusion.215) | copy-start | bytes 12292
  1980.5 21.4 copy-start.23
  2035.4 1496.2 %reduce-scatter.11.cloned.1.call-start = ((), (), s32[]{:S(2)}) async-start(), calls=%async_computation.11 | async-start | bytes 7208960 | tf_op jit(solution)/shard_map/reduce_scatter | solution.py:245
  2057.5 1474.1 %reduce-scatter.9.cloned.1.call-start = ((), (), s32[]{:S(2)}) async-start(), calls=%async_computation.10 | async-start | bytes 14417920 | tf_op jit(solution)/shard_map/reduce_scatter | solution.py:242
  2080.1 18.1 copy-start
  2145.5 19.1 copy-start
  2188.3 15.8 copy-start.1
  2211.9 19.1 copy-start
  2254.6 15.8 copy-start.1
  2278.3 19.1 copy-start
  2344.6 19.1 copy-start
  2387.3 15.8 copy-start.1
  2411.0 19.1 copy-start
  2477.3 19.1 copy-start
  2520.1 15.8 copy-start.1
  2543.7 19.1 copy-start
  2610.0 19.1 copy-start
  2652.8 15.8 copy-start.1
  2676.4 19.1 copy-start
  2742.7 19.1 copy-start
  2785.5 15.8 copy-start.1
  2809.1 19.1 copy-start
  2875.4 19.1 copy-start
  2941.8 19.1 copy-start
  3008.1 19.1 copy-start
  3074.4 19.1 copy-start
  3117.2 15.8 copy-start.1
  3142.2 21.0 copy-start.78
  3142.2 21.0 copy-start.88
  3183.1 413.9 %reduce-scatter.5.cloned.1.call-start = ((), (), s32[]{:S(2)}) async-start(), calls=%async_computation.8 | async-start | bytes 15728640 | tf_op jit(solution)/shard_map/reduce_scatter | solution.py:271
  3209.7 22.7 copy-start.33
  3209.7 39.6 slice-start.2
  3232.4 16.9 slice-start.3
  3361.8 44.9 %copy-start.60 = (f32[1,5120]{1,0:T(1,128)S(1)}, f32[1,5120]{1,0:T(1,128)}, u32[]{:S(2)}) copy-start(f32[1,5120]{1,0:T(1,128)} %copy-done.59) | copy-start | bytes 61444
  3361.8 44.9 %copy-start.62 = (f32[1,5120]{1,0:T(1,128)S(1)}, f32[1,5120]{1,0:T(1,128)}, u32[]{:S(2)}) copy-start(f32[1,5120]{1,0:T(1,128)} %copy-done.61) | copy-start | bytes 61444
  3361.8 44.9 %copy-start.64 = (f32[1,5120]{1,0:T(1,128)S(1)}, f32[1,5120]{1,0:T(1,128)}, u32[]{:S(2)}) copy-start(f32[1,5120]{1,0:T(1,128)} %copy-done.63) | copy-start | bytes 61444
  3361.8 44.9 %copy-start.66 = (f32[1,5120]{1,0:T(1,128)S(1)}, f32[1,5120]{1,0:T(1,128)}, u32[]{:S(2)}) copy-start(f32[1,5120]{1,0:T(1,128)} %get-tuple-element.932) | copy-start | bytes 61444
  3440.7 36.2 copy-start.18
  3440.7 36.2 copy-start.75
  3440.7 36.2 copy-start.84
  3496.8 229.7 %all-reduce.25.cloned.1.call-start = ((), (), s32[]{:S(2)}) async-start(), calls=%async_computation.12 | async-start | bytes 360448 | tf_op jit(solution)/shard_map/psum | solution.py:265
  3497.7 30.0 copy-start.48
  3528.7 68.4 %copy-start.94 = (f32[8]{0:T(128)S(1)}, f32[8]{0:T(128)}, u32[]{:S(2)}) copy-start(f32[8]{0:T(128)} %param.27) | copy-start | bytes 100
  3528.7 68.4 %copy-start.58 = (bf16[1024,24]{0,1:T(8,128)(2,1)S(1)}, bf16[1024,24]{0,1:T(8,128)(2,1)}, u32[]{:S(2)}) copy-start(bf16[1024,24]{0,1:T(8,128)(2,1)} %copy-done.57) | copy-start | bytes 147460
  3531.5 462.8 %all-reduce.27.cloned.1.call-start = ((), (), s32[]{:S(2)}) async-start(), calls=%async_computation.13 | async-start | bytes 15990784 | tf_op jit(solution)/shard_map/psum | solution.py:279
  3599.9 22.4 copy-start.86
  3599.9 22.4 copy-start.91
  3599.9 66.3 %copy-start.73 = (f32[1024]{0:T(1024)S(1)}, f32[1024]{0:T(1024)}, u32[]{:S(2)}) copy-start(f32[1024]{0:T(1024)} %copy-done.72) | copy-start | bytes 12292
  (273 other events, 1941.6 us)
Sparse Core Ops, SparseCore 0:
  9.6 84.7 all-gather.4
  96.0 22.5 all-gather.6
  120.2 76.1 all-gather.8
  197.8 43.3 all-gather.10
  2035.6 31.9 reduce-scatter.6
  2070.7 54.8 reduce-scatter.10
  3183.2 92.8 reduce-scatter.8
  3496.9 100.0 reduce-scatter.4
  3603.8 122.6 all-reduce.24
  3730.8 263.4 all-reduce.26
where the time goes:
time: 4050 us; the launch traced here: 4010 us
  other arithmetic  1700 us (42%)
  matrix products  992 us (24%)
  local copies, waits for them, and re-layouts  812 us (20%)
  waiting for transfers between devices  436 us (11%)
  blocking collectives  46.2 us (1%)
    another operation x4, other arithmetic, sequence_mix(): lax.linalg.triangular_solve(coupling, identity, left_side=True, lower=Tru...  1260 us
    psum x1, waiting for transfers between devices, shards(): lax.psum(own_in.astype(jnp.bfloat16), 'rep').astype(jnp.float32)  266 us
    dot_general x64, matrix products, block_step(): updates = jnp.einsum('hri,hid->hrd', inverse, targets, precision=PRECISE)  145 us
    dynamic_update_slice x128, local copies, waits for them, and re-layouts, sequence_mix(): final_memory, outputs = lax.scan(jax.checkpoint(block_step), memory, pieces)  144 us
    dot_general x64, matrix products, block_step(): jnp.einsum('htc,hic->hti', queries_head, keys_head, precision=PRECISE)  129 us
    dot_general x64, matrix products, block_step(): jnp.einsum('htc,hcd->htd', queries_head, memory, precision=PRECISE)  123 us
    dot_general x48, matrix products, block_step(): jnp.einsum('hic,hid->hcd', keys_head * carry_weights[:, :, None], updates...  119 us
    dot_general x64, matrix products, block_step(): carried = jnp.einsum('hrc,hcd->hrd', keys_head, memory, precision=PRECISE)  86.5 us
  transfers between devices with their start and end apart: 10, of which 4 were waited for; matrix products, arithmetic and copies ran while one was open for 84% of the time, Pallas kernels for 0%

commit v1 on v0

v1 whole, which is shorter than its diff:
```python
import functools

import jax
import jax.numpy as jnp
from jax import lax
from jax.experimental import pallas as pl
from jax.experimental.pallas import tpu as pltpu
from jax.sharding import PartitionSpec as P

HEADS = 8
DK = 128
HOUSE = 2
BLOCK = 64
HB = 4
GROUPS = HEADS // HB
EPSILON = 1e-06
EPS = EPSILON
f32 = jnp.float32
bf16 = jnp.bfloat16


def norm_rows(row_values, gain_row):
    return (
        row_values
        * lax.rsqrt(jnp.mean(row_values * row_values, axis=-1, keepdims=True) + EPSILON)
        * gain_row
    )


def dot_plain(a,b): return nn(a,b)
def dot_right_t(a,b): return nt(a,b)
def dot_left_t(a,b): return tn(a,b)
def nn(a,b): return lax.dot_general(a,b,(((1,),(0,)),((),())),preferred_element_type=f32)
def nt(a,b): return lax.dot_general(a,b,(((1,),(1,)),((),())),preferred_element_type=f32)
def tn(a,b): return lax.dot_general(a,b,(((0,),(0,)),((),())),preferred_element_type=f32)
def lo(x): return x.astype(bf16)
def sigmoid(x): return 0.5*jnp.tanh(0.5*x)+0.5
def cat(*xs): return jnp.concatenate(xs,axis=0)

def token_masks(C):
    row=lax.broadcasted_iota(jnp.int32,(C,2*C),0)
    col=lax.broadcasted_iota(jnp.int32,(C,2*C),1)
    left=col<C
    tok=jnp.where(left,col,col-C)
    return row,tok,left

def gates(colg,rowg,h,HB,C):
    c_col=colg[:,h:h+1]
    c_row=rowg[h:h+1,:]
    b_row=rowg[HB+h:HB+h+1,:]
    return c_col,c_row,b_row

def fwd_body(C,HB,x_ref,cw_ref,colg_ref,rowg_ref,nh_ref,mixed_ref,o_ref,s0_ref,t_ref,u_ref,xs,S):
    W=HB*128
    CV=5*W
    @pl.when(pl.program_id(2)==0)
    def _():
        xs[0:8,:]=jnp.zeros((8,CV),f32)
        S[...]=jnp.zeros_like(S)
    @pl.when(pl.program_id(2)!=0)
    def _():
        xs[0:8,:]=xs[C:C+8,:]
    xs[8:8+C,:]=x_ref[:,0:CV].astype(f32)
    row,tok,left=token_masks(C)
    incl=tok<=row
    strict=tok<row
    botm=tok<row+jnp.where(left,1,0)
    colg=colg_ref[...]
    rowg=rowg_ref[0]
    eye=jnp.where((tok==row)&left,1.0,0.0)
    eye2=jnp.where((tok==row)&jnp.logical_not(left),1.0,0.0)
    pair=jnp.where((tok==row)&left,1.0,0.0)
    def act(slot,h):
        sl=slice(slot*W+h*128,slot*W+h*128+128)
        y=cw_ref[3:4,sl]*xs[8:8+C,sl]
        for i in range(3):
            y=y+cw_ref[i:i+1,sl]*xs[5+i:5+i+C,sl]
        return y*sigmoid(y)
    def l2(a): return a*lax.rsqrt(jnp.sum(a*a,axis=-1,keepdims=True)+EPS)
    H=range(HB)
    Q=[];K=[];V=[];E=[];G3=[]
    for h in H:
        q=l2(act(0,h))*(128**-0.5)
        k=cat(l2(act(1,h)),l2(act(2,h)))
        Q.append(q);K.append(k)
        V.append(cat(act(3,h),act(4,h)))
    Y=[lo(cat(Q[h],K[h])) for h in H]
    Kb=[lo(K[h]) for h in H]
    GP=[nt(Y[h],Kb[h]) for h in H]
    A=[];M=[];CC=[]
    for h in H:
        c_col,c_row,b_row=gates(colg,rowg,h,HB,C)
        e=jnp.exp(jnp.minimum(c_col-c_row,0.0))*b_row
        M.append(lo(jnp.where(incl,GP[h][0:C]*e,0.0)))
        A.append(cat(jnp.where(strict,GP[h][C:2*C]*e,0.0),jnp.where(botm,GP[h][2*C:3*C]*e,0.0)))
    T=[cat(eye,eye2-A[h][C:2*C]*pair) for h in H]
    s=1
    while s<C:
        m=((tok//(2*s))==(row//(2*s)))&((row//s)%2==1)&((tok//s)%2==0)
        mf=jnp.where(m,1.0,0.0)
        Tb=[lo(T[h]) for h in H]
        Z=[nn(lo(cat(A[h][0:C]*mf,A[h][C:2*C]*mf)),Tb[h]) for h in H]
        T=[T[h]-nn(Tb[h],lo(Z[h])) for h in H]
        s*=2
    Tb=[lo(T[h]) for h in H]
    S0=[S[:,h*128:h*128+128] for h in H]
    S0b=[lo(S0[h]) for h in H]
    YS=[nn(Y[h],S0b[h]) for h in H]
    U=[]
    for h in H:
        c_col=colg[:,h:h+1]
        ec=jnp.exp(c_col)
        ks=YS[h][C:3*C]
        R=V[h]-cat(ec*ks[0:C],ec*ks[C:2*C])
        U.append(lo(nn(Tb[h],lo(R))))
    for h in H:
        sl=slice(h*128,h*128+128)
        c_col=colg[:,h:h+1]
        ec=jnp.exp(c_col)
        O=ec*YS[h][0:C]+nn(M[h],U[h])
        cl=colg[C-1:C,h:h+1]
        ew=jnp.exp(cl-c_col)
        w0=ew*colg[:,HB+h:HB+h+1]
        w1=ew*colg[:,2*HB+h:2*HB+h+1]
        kw=lo(cat(w0*K[h][0:C],w1*K[h][C:2*C]))
        S[:,sl]=jnp.exp(cl)*S0[h]+tn(kw,U[h])
        s0_ref[0,:,sl]=S0b[h]
        t_ref[0,:,sl]=Tb[h]
        u_ref[0,:,sl]=U[h]
        o_ref[:,sl]=O
        g=x_ref[:,CV+h*128:CV+h*128+128].astype(f32)
        r=lax.rsqrt(jnp.mean(O*O,axis=-1,keepdims=True)+EPS)
        mixed_ref[:,sl]=lo(O*r*nh_ref[...]*(g*sigmoid(g)))

def mixer_fwd(x,cw,colg,rowg,nh,nseq):
    C=BLOCK
    R=x.shape[0]; nch=R//nseq//C; W=HB*128; ng=GROUPS
    rb=lambda g,s,n:(s*nch+n,g)
    cb=lambda g,s,n:(s*nch+n,0,g)
    NC=nseq*nch
    return pl.pallas_call(
        functools.partial(fwd_body,C,HB),
        grid=(ng,nseq,nch),
        in_specs=[pl.BlockSpec((C,6*W),rb),pl.BlockSpec((4,5*W),lambda g,s,n:(0,g)),
                  pl.BlockSpec((C,128),rb),pl.BlockSpec((1,2*HB,128),lambda g,s,n:(s*nch+n,g,0)),
                  pl.BlockSpec((1,128),lambda g,s,n:(0,0))],
        out_specs=[pl.BlockSpec((C,W),rb),pl.BlockSpec((C,W),rb),
                   pl.BlockSpec((1,128,W),cb),pl.BlockSpec((1,128,W),cb),pl.BlockSpec((1,128,W),cb)],
        out_shape=[jax.ShapeDtypeStruct((R,ng*W),bf16),jax.ShapeDtypeStruct((R,ng*W),f32),
                   jax.ShapeDtypeStruct((NC,128,ng*W),bf16),jax.ShapeDtypeStruct((NC,128,ng*W),bf16),jax.ShapeDtypeStruct((NC,128,ng*W),bf16)],
        scratch_shapes=[pltpu.VMEM((C+8,5*W),f32),pltpu.VMEM((128,W),f32)],
        compiler_params=pltpu.CompilerParams(dimension_semantics=("arbitrary",)*3,vmem_limit_bytes=48<<20),
        name="mixer_fwd",
    )(x,cw,colg,rowg,nh)

def bwd_body(C,HB,x_ref,xp_ref,cw_ref,colg_ref,rowg_ref,nh_ref,gm_ref,o_ref,s0_ref,t_ref,u_ref,
             gx_ref,col_ref,row_ref,dcw_ref,dnh_ref,xs,gs,dS):
    W=HB*128
    CV=5*W
    n=pl.program_id(2); nch=pl.num_programs(2)
    first=(pl.program_id(1)==0)&(n==0)
    @pl.when(first)
    def _():
        dcw_ref[...]=jnp.zeros_like(dcw_ref)
        dnh_ref[...]=jnp.zeros_like(dnh_ref)
    @pl.when(n==0)
    def _():
        gs[C:C+8,:]=jnp.zeros((8,CV),f32)
        dS[...]=jnp.zeros_like(dS)
    @pl.when(n!=0)
    def _():
        gs[C:C+8,:]=gs[0:8,:]
    @pl.when(n==nch-1)
    def _():
        xs[0:8,:]=jnp.zeros((8,CV),f32)
    @pl.when(n!=nch-1)
    def _():
        xs[0:8,:]=xp_ref[:,0:CV].astype(f32)
    xs[8:8+C,:]=x_ref[:,0:CV].astype(f32)
    row,tok,left=token_masks(C)
    incl=tok<=row
    strict=tok<row
    botm=tok<row+jnp.where(left,1,0)
    colg=colg_ref[...]
    rowg=rowg_ref[0]
    lane=lax.broadcasted_iota(jnp.int32,(C,128),1)
    H=range(HB)
    def conv(slot,h):
        sl=slice(slot*W+h*128,slot*W+h*128+128)
        y=cw_ref[3:4,sl]*xs[8:8+C,sl]
        for i in range(3):
            y=y+cw_ref[i:i+1,sl]*xs[5+i:5+i+C,sl]
        return y
    def act_norm(slot,h):
        y=conv(slot,h)
        sg=sigmoid(y)
        a=y*sg
        r=lax.rsqrt(jnp.sum(a*a,axis=-1,keepdims=True)+EPS)
        dsil=sg*(1.0+y*(1.0-sg))
        return a*r,r,dsil
    Q=[];K=[];rq=[];rk0=[];rk1=[];dq_s=[];dk0_s=[];dk1_s=[]
    for h in H:
        a,r,d=act_norm(0,h); Q.append(a*(128**-0.5)); rq.append(r); dq_s.append(d)
        a0,r0,d0=act_norm(1,h); a1,r1,d1=act_norm(2,h)
        K.append(cat(a0,a1)); rk0.append(r0); rk1.append(r1); dk0_s.append(d0); dk1_s.append(d1)
    dO=[]
    nhg=nh_ref[...]
    for h in H:
        sl=slice(h*128,h*128+128)
        O=o_ref[:,sl]; gm=gm_ref[:,sl].astype(f32)
        gt=x_ref[:,CV+h*128:CV+h*128+128].astype(f32)
        sg=sigmoid(gt)
        r=lax.rsqrt(jnp.mean(O*O,axis=-1,keepdims=True)+EPS)
        on=O*r
        gsil=gm*(gt*sg)
        t1=gsil*on
        dnh_ref[0]+=jnp.sum(t1.reshape(C//8,8,128),axis=0)
        dgt=gm*(on*nhg)*(sg*(1.0+gt*(1.0-sg)))
        gx_ref[:,CV+h*128:CV+h*128+128]=lo(dgt)
        u=gsil*nhg
        dO.append(r*(u-on*jnp.mean(u*on,axis=-1,keepdims=True)))
    Y=[cat(Q[h],K[h]) for h in H]
    Yb=[lo(y) for y in Y]
    Kb=[lo(K[h]) for h in H]
    GP=[nt(Yb[h],Kb[h]) for h in H]
    dU=[];Eq=[];EA=[];dSb=[];ecs=[];ews=[]
    for h in H:
        sl=slice(h*128,h*128+128)
        c_col,c_row,b_row=gates(colg,rowg,h,HB,C)
        e=jnp.exp(jnp.minimum(c_col-c_row,0.0))
        eq=jnp.where(incl,e,0.0); ea=cat(jnp.where(strict,e,0.0),jnp.where(botm,e,0.0))
        Eq.append(eq);EA.append(ea)
        M=lo(GP[h][0:C]*eq*b_row)
        cl=colg[C-1:C,h:h+1]
        ec=jnp.exp(c_col); ew=jnp.exp(cl-c_col)
        ecs.append(ec);ews.append(ew)
        w0=ew*colg[:,HB+h:HB+h+1]
        w1=ew*colg[:,2*HB+h:2*HB+h+1]
        kw=lo(cat(w0*K[h][0:C],w1*K[h][C:2*C]))
        db_=lo(dS[:,sl]); dSb.append(db_)
        dU.append(lo(tn(M,lo(dO[h]))+nn(kw,db_)))
    dR=[tn(t_ref[0,:,h*128:h*128+128],dU[h]) for h in H]
    dAM=[nt(lo(cat(dO[h],-dR[h])),u_ref[0,:,h*128:h*128+128]) for h in H]
    Z=[]
    for h in H:
        ec=ecs[h]
        Z.append(lo(cat(ec*dO[h],-(ec*dR[h][0:C]),-(ec*dR[h][C:2*C]))))
    UdS=[nt(u_ref[0,:,h*128:h*128+128],dSb[h]) for h in H]
    colout=jnp.zeros((C,128),f32)
    rows=[]
    X=[]
    ZS=[nt(Z[h],s0_ref[0,:,h*128:h*128+128]) for h in H]
    for h in H:
        sl=slice(h*128,h*128+128)
        cl=colg[C-1:C,h:h+1]
        b_row=rowg[HB+h:HB+h+1,:]
        S0f=s0_ref[0,:,sl].astype(f32)
        dSf=dS[:,sl]
        dSS=jnp.sum(dSf*S0f,axis=0,keepdims=True)*jnp.exp(cl)
        dS[:,sl]=jnp.exp(cl)*dSf+tn(Yb[h],Z[h])
        dM=dAM[h][0:C]; dA=dAM[h][C:3*C]
        xm=dM*Eq[h]; xa=dA*EA[h]
        XM=xm*GP[h][0:C]; XA=xa*GP[h][C:3*C]
        cs=jnp.sum(XM,axis=0,keepdims=True)+jnp.sum(XA,axis=0,keepdims=True)
        rows.append((cs,b_row*cs,dSS))
        XMb=XM*b_row
        XAb=XA*b_row
        rs=jnp.sum(XMb+XAb[0:C]+XAb[C:2*C],axis=-1,keepdims=True)
        yz=Y[h]*ZS[h]
        rs=rs+jnp.sum(yz[0:C]+yz[C:2*C]+yz[2*C:3*C],axis=-1,keepdims=True)
        ku=K[h]*UdS[h]
        d0=ews[h]*jnp.sum(ku[0:C],axis=-1,keepdims=True)
        d1=ews[h]*jnp.sum(ku[C:2*C],axis=-1,keepdims=True)
        colout=jnp.where(lane==h,rs,colout)
        colout=jnp.where(lane==HB+h,d0,colout)
        colout=jnp.where(lane==2*HB+h,d1,colout)
        X.append(lo(cat(xm*b_row,xa[0:C]*b_row,xa[C:2*C]*b_row)))
    col_ref[...]=colout
    row_ref[0]=jnp.concatenate([rows[h][i] for i in range(3) for h in H]+[jnp.zeros((16-3*HB,128),f32)],axis=0)
    XK=[nn(X[h],Kb[h]) for h in H]
    XY=[tn(X[h],Yb[h]) for h in H]
    def l2b(g,nrm,r):
        return r*(g-nrm*jnp.sum(g*nrm,axis=-1,keepdims=True))
    for h in H:
        ew=ews[h]
        w0=ew*colg[:,HB+h:HB+h+1]
        w1=ew*colg[:,2*HB+h:2*HB+h+1]
        sl=lambda s: slice(s*W+h*128,s*W+h*128+128)
        dq=ZS[h][0:C]+XK[h][0:C]
        dk=ZS[h][C:3*C]+XK[h][C:3*C]+XY[h]
        dk0=dk[0:C]+w0*UdS[h][0:C]
        dk1=dk[C:2*C]+w1*UdS[h][C:2*C]
        gs[0:C,sl(0)]=l2b(dq*(128**-0.5),Q[h]*(128**0.5),rq[h])*dq_s[h]
        gs[0:C,sl(1)]=l2b(dk0,K[h][0:C],rk0[h])*dk0_s[h]
        gs[0:C,sl(2)]=l2b(dk1,K[h][C:2*C],rk1[h])*dk1_s[h]
        for j in range(2):
            y=conv(3+j,h); sg=sigmoid(y)
            gs[0:C,sl(3+j)]=dR[h][j*C:j*C+C]*(sg*(1.0+y*(1.0-sg)))
        for s in range(5):
            g=gs[0:C,sl(s)]
            gx=cw_ref[3:4,sl(s)]*g
            dcw_ref[3,:,sl(s)]+=jnp.sum((g*xs[8:8+C,sl(s)]).reshape(C//8,8,128),axis=0)
            for i in range(3):
                gx=gx+cw_ref[i:i+1,sl(s)]*gs[3-i:3-i+C,sl(s)]
                dcw_ref[i,:,sl(s)]+=jnp.sum((g*xs[5+i:5+i+C,sl(s)]).reshape(C//8,8,128),axis=0)
            gx_ref[:,sl(s)]=lo(gx)

def mixer_bwd(x,cw,colg,rowg,nh,gm,o,s0,t,u,nseq):
    C=BLOCK
    R=x.shape[0]; nch=R//nseq//C; W=HB*128; ng=GROUPS
    ch=lambda s,n: s*nch+nch-1-n
    rb=lambda g,s,n:(ch(s,n),g)
    cb=lambda g,s,n:(ch(s,n),0,g)
    NC=nseq*nch
    return pl.pallas_call(
        functools.partial(bwd_body,C,HB),
        grid=(ng,nseq,nch),
        in_specs=[pl.BlockSpec((C,6*W),rb),
                  pl.BlockSpec((8,6*W),lambda g,s,n:(jnp.maximum(ch(s,n)*(C//8)-1,0),g)),
                  pl.BlockSpec((4,5*W),lambda g,s,n:(0,g)),
                  pl.BlockSpec((C,128),rb),pl.BlockSpec((1,2*HB,128),lambda g,s,n:(ch(s,n),g,0)),
                  pl.BlockSpec((1,128),lambda g,s,n:(0,0)),
                  pl.BlockSpec((C,W),rb),pl.BlockSpec((C,W),rb),
                  pl.BlockSpec((1,128,W),cb),pl.BlockSpec((1,128,W),cb),pl.BlockSpec((1,128,W),cb)],
        out_specs=[pl.BlockSpec((C,6*W),rb),pl.BlockSpec((C,128),rb),
                   pl.BlockSpec((1,16,128),lambda g,s,n:(ch(s,n),g,0)),
                   pl.BlockSpec((4,8,5*W),lambda g,s,n:(0,0,g)),
                   pl.BlockSpec((1,8,128),lambda g,s,n:(g,0,0))],
        out_shape=[jax.ShapeDtypeStruct((R,ng*6*W),bf16),jax.ShapeDtypeStruct((R,ng*128),f32),
                   jax.ShapeDtypeStruct((NC,ng*16,128),f32),
                   jax.ShapeDtypeStruct((4,8,ng*5*W),f32),jax.ShapeDtypeStruct((ng,8,128),f32)],
        scratch_shapes=[pltpu.VMEM((C+8,5*W),f32),pltpu.VMEM((C+8,5*W),f32),pltpu.VMEM((128,W),f32)],
        compiler_params=pltpu.CompilerParams(dimension_semantics=("arbitrary",)*3,vmem_limit_bytes=48<<20),
        name="mixer_bwd",
    )(x,x,cw,colg,rowg,nh,gm,o,s0,t,u)

def make_gates(small,a_log,dt_bias):
    C=BLOCK
    R=small.shape[0]; NC=R//C; ng=8//HB
    beta=jax.nn.sigmoid(small[:,:16])
    pre=small[:,16:24]+dt_bias
    g=-jnp.exp(a_log)*jax.nn.softplus(pre)
    c=jnp.cumsum(g.reshape(NC,C,8),axis=1)
    cf=c.reshape(R,8)
    gr=lambda z: z.reshape(R,ng,HB)
    colg=jnp.concatenate([gr(cf),gr(beta[:,:8]),gr(beta[:,8:]),jnp.zeros((R,ng,128-3*HB),f32)],axis=2).reshape(R,ng*128)
    ct=c.transpose(0,2,1)
    crow=jnp.concatenate([ct,ct],axis=2).reshape(NC,ng,HB,2*C)
    b=beta.reshape(NC,C,2,8).transpose(0,3,2,1).reshape(NC,ng,HB,2*C)
    rowg=jnp.concatenate([crow,b],axis=2).reshape(NC,ng*2*HB,2*C)
    return colg,rowg,(beta,pre,g)

def gates_bwd(col,row,saved,a_log):
    C=BLOCK
    beta,pre,g=saved
    R=beta.shape[0]; NC=R//C; ng=8//HB
    co=col.reshape(R,ng,128)
    rs=co[:,:,:HB].reshape(NC,C,8)
    d0=co[:,:,HB:2*HB].reshape(R,8); d1=co[:,:,2*HB:3*HB].reshape(R,8)
    ro=row.reshape(NC,ng,16,128)
    tr=lambda z: z.reshape(NC,8,2,C).transpose(0,3,2,1)
    cs=tr(ro[:,:,:HB]); csb=tr(ro[:,:,HB:2*HB]); dss=jnp.sum(ro[:,:,2*HB:3*HB],axis=-1).reshape(NC,8)
    dw=jnp.stack([d0,d1],axis=1)
    dbeta=cs.reshape(R,2,8)+dw
    bdw=(beta.reshape(R,2,8)*dw).reshape(NC,C,2,8)
    dc=rs-jnp.sum(csb+bdw,axis=2)
    dcl=dss+jnp.sum(bdw,axis=(1,2))
    dg=lax.cumsum(dc,axis=1,reverse=True)+dcl[:,None,:]
    dg=dg.reshape(R,8)
    dbeta=dbeta.reshape(R,16)
    dsmall_b=dbeta*beta*(1.0-beta)
    dpre=dg*(-jnp.exp(a_log))*jax.nn.sigmoid(pre)
    g_alog=jnp.sum(dg*g,axis=0)
    g_dtb=jnp.sum(dpre,axis=0)
    return jnp.concatenate([dsmall_b,dpre],axis=1),g_alog,g_dtb


def to_groups(w):
    rows = w.shape[0]
    return w.reshape(rows, 6, GROUPS, HB * DK).transpose(0, 2, 1, 3).reshape(rows, w.shape[1])


def from_groups(w):
    rows = w.shape[0]
    return w.reshape(rows, GROUPS, 6, HB * DK).transpose(0, 2, 1, 3).reshape(rows, w.shape[1])


def all_sum(vec, total):
    axes = ("rep", "shard")
    step = 1
    while step < total:
        vec = vec + lax.ppermute(vec, axes, [(i, i ^ step) for i in range(total)])
        step *= 2
    return vec


def gather(w):
    return lax.all_gather(w, "shard", axis=0, tiled=True)


def scatter(w):
    return lax.psum_scatter(w, "shard", scatter_dimension=0, tiled=True)


def shards(
    total,
    hidden_in,
    teacher,
    cotangent,
    lengths,
    norm_attn,
    w_in,
    w_small,
    conv_w,
    a_log,
    dt_bias,
    norm_head,
    w_out,
    norm_mlp,
    w_mlp_in,
    w_mlp_down,
):
    row_count, width = hidden_in.shape
    seq_here = lengths.shape[0]
    slot_count = row_count // seq_here
    small_width = w_small.shape[1]
    proj_width = w_in.shape[1]
    wide = jnp.concatenate(
        [to_groups(w_in), jnp.pad(w_small, ((0, 0), (0, 128 - small_width)))], axis=1
    )
    wide_all = gather(wide)
    w_out_all = gather(w_out)
    w_mlp_in_all = gather(w_mlp_in)
    w_down_all = gather(w_mlp_down)

    hidden32 = hidden_in.astype(f32)
    r_in = lax.rsqrt(jnp.mean(hidden32 * hidden32, axis=-1, keepdims=True) + EPSILON)
    normed_low = (hidden32 * r_in * norm_attn).astype(bf16)
    proj = dot_plain(normed_low, wide_all)
    small = proj[:, proj_width : proj_width + small_width]
    conv_pad = jnp.pad(conv_w, ((0, 0), (0, proj_width - conv_w.shape[1])))
    conv_groups = to_groups(conv_pad).reshape(4, GROUPS, 6 * HB * DK)[:, :, : 5 * HB * DK]
    conv_groups = conv_groups.reshape(4, GROUPS * 5 * HB * DK)
    head_gain = norm_head.reshape(1, DK)
    colg, rowg, saved = make_gates(small, a_log, dt_bias)
    mixed_low, heads_out, states, inverses, updates = mixer_fwd(
        proj, conv_groups, colg, rowg, head_gain, seq_here
    )
    residual = hidden32 + dot_plain(mixed_low, w_out_all)
    r_mid = lax.rsqrt(jnp.mean(residual * residual, axis=-1, keepdims=True) + EPSILON)
    mid_low = (residual * r_mid * norm_mlp).astype(bf16)
    gate_up = dot_plain(mid_low, w_mlp_in_all)
    unit_count = w_down_all.shape[0]
    gate_part = gate_up[:, :unit_count]
    up_part = gate_up[:, unit_count:]
    sigmoid_gate = jax.nn.sigmoid(gate_part)
    silu_gate = gate_part * sigmoid_gate
    product_low = (silu_gate * up_part).astype(bf16)
    output32 = residual + dot_plain(product_low, w_down_all)
    slot_index = lax.broadcasted_iota(jnp.int32, (seq_here, slot_count), 1)
    valid_rows = (slot_index < lengths[:, None]).astype(f32).reshape(row_count, 1)
    deviation = output32 - teacher.astype(f32)
    loss_sum = jnp.sum(valid_rows * deviation * deviation)
    valid_count = jnp.sum(lengths).astype(f32)
    grad_out = valid_rows * (cotangent.astype(f32) + deviation)
    grad_out_low = grad_out.astype(bf16)

    grad_w_down = dot_left_t(product_low, grad_out_low).astype(bf16)
    own_down = scatter(grad_w_down)
    grad_product = dot_right_t(grad_out_low, w_down_all)
    grad_gate = grad_product * up_part * sigmoid_gate * (1.0 + gate_part * (1.0 - sigmoid_gate))
    grad_up = grad_product * silu_gate
    grad_gate_up = jnp.concatenate([grad_gate, grad_up], axis=1).astype(bf16)
    grad_w_mlp_in = dot_left_t(mid_low, grad_gate_up).astype(bf16)
    own_mlp_in = scatter(grad_w_mlp_in)
    grad_mid = dot_right_t(grad_gate_up, w_mlp_in_all)
    u_mid = grad_mid * norm_mlp
    grad_norm_mlp = jnp.sum(grad_mid * residual * r_mid, axis=0)
    grad_residual = (
        grad_out
        + r_mid * u_mid
        - (r_mid * r_mid * r_mid) * residual * jnp.mean(u_mid * residual, axis=-1, keepdims=True)
    )
    grad_res_low = grad_residual.astype(bf16)
    grad_mixed = dot_right_t(grad_res_low, w_out_all)
    grad_w_out = dot_left_t(mixed_low, grad_res_low).astype(bf16)
    own_out = scatter(grad_w_out)
    own_down, own_mlp_in, own_out = lax.psum((own_down, own_mlp_in, own_out), "rep")

    grad_proj_low, col_out, row_out, conv_out, gain_out = mixer_bwd(
        proj, conv_groups, colg, rowg, head_gain, grad_mixed, heads_out, states, inverses,
        updates, seq_here,
    )
    grad_small, grad_log, grad_bias = gates_bwd(col_out, row_out, saved, a_log)
    grad_small_low = jnp.pad(grad_small.astype(bf16), ((0, 0), (0, 128 - small_width)))
    grad_wide = jnp.concatenate(
        [dot_left_t(normed_low, grad_proj_low), dot_left_t(normed_low, grad_small_low)], axis=1
    ).astype(bf16)
    own_wide = scatter(grad_wide)
    own_wide, own_down, own_mlp_in, own_out = lax.optimization_barrier(
        (own_wide, own_down, own_mlp_in, own_out)
    )
    own_wide = lax.psum(own_wide, "rep").astype(f32)
    grad_normed = dot_right_t(grad_proj_low, wide_all[:, :proj_width]) + dot_right_t(
        grad_small_low, wide_all[:, proj_width:]
    )
    u_in = grad_normed * norm_attn
    grad_norm_attn = jnp.sum(grad_normed * hidden32 * r_in, axis=0)
    grad_hidden = (
        grad_residual
        + r_in * u_in
        - (r_in * r_in * r_in) * hidden32 * jnp.mean(u_in * hidden32, axis=-1, keepdims=True)
    ).astype(bf16)

    grad_conv = jnp.sum(conv_out, axis=1).reshape(4, GROUPS, 5, HB * DK)
    grad_conv = grad_conv.transpose(0, 2, 1, 3).reshape(4, conv_w.shape[1])
    grad_gain = jnp.sum(gain_out, axis=(0, 1))
    parts = (
        grad_norm_attn,
        grad_conv.reshape(-1),
        grad_norm_mlp,
        grad_gain,
        grad_log,
        grad_bias,
        loss_sum.reshape(1),
        valid_count.reshape(1),
        jnp.zeros((110,), f32),
    )
    packed = jnp.concatenate(parts).reshape(-1, 128)
    packed = all_sum(packed, total).reshape(-1)
    sums = []
    start = 0
    for part in parts:
        sums.append(packed[start : start + part.shape[0]])
        start += part.shape[0]
    loss_value = sums[6][0] / (sums[7][0] * width)
    return (
        output32.astype(bf16),
        loss_value,
        grad_hidden,
        sums[0],
        from_groups(own_wide[:, :proj_width]),
        own_wide[:, proj_width : proj_width + small_width],
        sums[1].reshape(conv_w.shape),
        sums[4],
        sums[5],
        sums[3],
        own_out.astype(f32),
        sums[2],
        own_mlp_in.astype(f32),
        own_down.astype(f32),
    )


def solution(mesh):
    total = mesh.shape["rep"] * mesh.shape["shard"]
    in_specs = (
        P(("rep", "shard"), None),
        P(("rep", "shard"), None),
        P(("rep", "shard"), None),
        P(("rep", "shard")),
        P(),
        P("shard", None),
        P("shard", None),
        P(),
        P(),
        P(),
        P(),
        P("shard", None),
        P(),
        P("shard", None),
        P("shard", None),
    )
    out_specs = (
        P(("rep", "shard"), None),
        P(),
        P(("rep", "shard"), None),
        P(),
        P("shard", None),
        P("shard", None),
        P(),
        P(),
        P(),
        P(),
        P("shard", None),
        P(),
        P("shard", None),
        P("shard", None),
    )
    return jax.shard_map(
        functools.partial(shards, total),
        mesh=mesh,
        in_specs=in_specs,
        out_specs=out_specs,
        check_vma=False,
    )
```

time: 4050 us -> 992 us (0.24)
  other arithmetic: 1700 us -> 62.9 us
  matrix products: 992 us -> 195 us
  local copies, waits for them, and re-layouts: 812 us -> 70.7 us
  Pallas kernels: 0 us -> 196 us
  blocking collectives: 46.2 us -> 0 us
    another operation x87 -> x3, other arithmetic: 1330 us -> 8.76 us  [the longest x1 6.33 us: make_gates(): c = jnp.cumsum(g.reshape(NC, C, 8), axis=1)]
    dot_general x371 -> x14, matrix products: 953 us -> 195 us  [the longest x5 74.5 us: nt(): lax.dot_general(a, b, (((1,), (1,)), ((), ())), preferred_element_type=f32)]
    pallas_call x0 -> x2, Pallas kernels: none -> 196 us  [the longest x1 105 us: mixer_bwd(): pl.pallas_call(functools.partial(bwd_body, C, HB), grid=(ng, nseq, nch),...]
    dynamic_update_slice x128 -> x0, local copies, waits for them, and re-layouts: 144 us -> none  [sequence_mix(): final_memory, outputs = lax.scan(jax.checkpoint(block_step), memory, pieces)]
    mul x186 -> x0, local copies, waits for them, and re-layouts: 129 us -> none  [the longest x48 48.3 us: block_step(): jnp.einsum('htc,hic->hti', queries_head, keys_head, precision=PRECISE)]
    mul x25 -> x3, other arithmetic: 121 us -> 0.9 us  [the longest x1 0.8 us: shards(): r_in * r_in * r_in]
    add_any x39 -> x0, other arithmetic: 93.1 us -> none  [the longest x2 36.8 us: mixer_core(): conv_out = conv_w[0] * padded[0:slot_count]]
    squeeze x96 -> x0, local copies, waits for them, and re-layouts: 85.5 us -> none  [the longest x64 77.4 us: sequence_mix(): final_memory, outputs = lax.scan(jax.checkpoint(block_step), memory, pieces)]
  transfers between devices with their start and end apart: 10 -> 15, of which waited for: 4 -> 8; matrix products, arithmetic and copies ran while one was open for 84% -> 23% of each run, Pallas kernels for 0% -> 20%
where the time goes in v1:
time: 992 us; the launch traced here: 983 us
  waiting for transfers between devices  437 us (44%)
  Pallas kernels  196 us (20%)
  matrix products  195 us (20%)
  local copies, waits for them, and re-layouts  70.7 us (7%)
  other arithmetic  62.9 us (6%)
  between operations  18.4 us (2%)
    psum x1, waiting for transfers between devices, shards(): lax.psum((own_down, own_mlp_in, own_out), 'rep')  178 us
    pallas_call x1, Pallas kernels, mixer_bwd(): pl.pallas_call(functools.partial(bwd_body, C, HB), grid=(ng, nseq, nch),...  105 us
    reduce_scatter x4, waiting for transfers between devices, scatter(): return lax.psum_scatter(w, 'shard', scatter_dimension=0, tiled=True)  100 us
    pallas_call x1, Pallas kernels, mixer_fwd(): pl.pallas_call(functools.partial(fwd_body, C, HB), grid=(ng, nseq, nch),...  91 us
    dot_general x5, matrix products, nt(): lax.dot_general(a, b, (((1,), (1,)), ((), ())), preferred_element_type=f32)  74.5 us
    all_gather x4, waiting for transfers between devices, gather(): return lax.all_gather(w, 'shard', axis=0, tiled=True)  74.2 us
    dot_general x4, matrix products, nn(): lax.dot_general(a, b, (((1,), (0,)), ((), ())), preferred_element_type=f32)  64 us
    psum x1, waiting for transfers between devices, shards(): own_wide = lax.psum(own_wide, 'rep').astype(f32)  63.9 us
  transfers between devices with their start and end apart: 15, of which 8 were waited for; matrix products, arithmetic and copies ran while one was open for 23% of the time, Pallas kernels for 20%

profile of v1, /device:TPU:0, one launch (start us, length us, event | category | flops | bytes accessed | tf_op | source)
XLA Modules:
  0.0 982.9 jit_solution(2673731262767015988)
XLA Ops:
  7.2 3.2 copy.219
  11.1 1.9 fusion.15
  13.1 0.7 all-gather.7.cloned.1.call-update
  15.2 2.6 copy.233
  17.7 3.9 copy.232
  22.4 3.1 copy.218
  25.9 0.8 multiply_multiply_fusion.1
  27.0 74.2 %all-gather.5.cloned.1.call-done = bf16[1024,6272]{0,1:T(8,128)(2,1)} async-done(((bf16[256,6272]{0,1:T(8,128)(2,1)}), bf16[1024,6272]{0,1:T(8,128)(2,1)}) %all-gather.5.cloned.1.call-update) | async-done | bytes 12845072 | tf_op jit(solution)/shard_map/all_gather | solution.py:398
  101.2 22.5 %fusion.48.x_ref.xp_ref = f32[1024,6272]{1,0:T(8,128)} fusion(bf16[1024,6272]{0,1:T(8,128)(2,1)} %all-gather.5.cloned.1.call-done, bf16[1024,1024]{0,1:T(8,128)(2,1)S(1)} %copy.218, f32[1024]{0:T(1024)S(1)} %copy-done.25, f32[1024]{0:T(1024)S(1)} %get-tuple-element.158), kind=kOutput, calls=%fused_computation.100 | convolution fusion | flops 13157531648 | bytes 40640512 | tf_op jit(solution)/shard_map/dot_general | solution.py:33
  123.8 1.1 slice.118
  124.8 1.2 slice.117
  129.2 6.3 fusion.56
  135.9 1.4 copy.225
  137.4 3.6 maximum_maximum_fusion
  141.9 91.0 %mixer_fwd.1 = (bf16[1024,1024]{1,0:T(8,128)(2,1)S(1)}, f32[1024,1024]{1,0:T(8,128)}, bf16[16,128,1024]{2,1,0:T(8,128)(2,1)}, bf16[16,128,1024]{2,1,0:T(8,128)(2,1)}, bf16[16,128,1024]{2,1,0:T(8,128)(2,1)}) custom-call(f32[1024,6272]{1,0:T(8,128)} %fusion.48.x_ref.xp_ref, f32[4,5120]{1,0:T(4,128)S(1)} %bitcast.118, f32[1024,256]{1,0:T(8,128)S(1)} %bitcast.114, ...), custom_call_target="tpu_custom_call" | custom-call | tf_op jit(solution)/shard_map/mixer_fwd/pallas_call | solution.py:141
  233.6 6.8 multiply_reduce_fusion.2
  240.5 21.2 %fusion.45 = f32[1024,5632]{1,0:T(8,128)} fusion(bf16[1024,5632]{1,0:T(8,128)(2,1)} %all-gather.9.cloned.1.call-done, f32[1024,1024]{0,1:T(8,128)} %get-tuple-element.162, f32[1024]{0:T(1024)S(1)} %copy-done.29, f32[1024]{0:T(1024)S(1)} %get-tuple-element.160), kind=kOutput, calls=%fused_computation.99 | convolution fusion | flops 11814305792 | bytes 38805504 | tf_op jit(solution)/shard_map/dot_general | solution.py:33
  261.7 11.6 %multiply_convert_fusion.2 = bf16[1024,2816]{1,0:T(8,128)(2,1)} fusion(f32[1024,5632]{1,0:T(8,128)} %fusion.45), kind=kLoop, calls=%fused_computation.6 | loop fusion | flops 17301504 | bytes 28835840 | tf_op jit(solution)/shard_map/convert_element_type | solution.py:458
  273.2 13.5 %fusion.16 = (bf16[1024,1024]{0,1:T(8,128)(2,1)}, f32[1024,1024]{0,1:T(8,128)}) fusion(bf16[1024,1024]{0,1:T(8,128)(2,1)} %copy.233, bf16[1024,1024]{0,1:T(8,128)(2,1)} %copy.232, f32[1024]{0:T(1024)S(1)} %fusion.36, f32[1024,1024]{0,1:T(8,128)} %get-tuple-element.162, bf16[1024,2816]{1,0:T(8,128)(2,1)} %multiply_convert_fusion.2, ...), kind=kOutput, calls=%fused_computation.43 | convolution fusion | flops 5912920064 | bytes 26218496 | tf_op jit(solution)/shard_map/dot_general | solution.py:33
  286.7 20.6 %multiply_convert_fusion.1 = (bf16[1024,2816]{1,0:T(8,128)(2,1)}, bf16[1024,2816]{1,0:T(8,128)(2,1)}) fusion(f32[1024,5632]{1,0:T(8,128)} %fusion.45, bf16[1024,1024]{0,1:T(8,128)(2,1)} %get-tuple-element.163, bf16[2816,1024]{1,0:T(8,128)(2,1)} %all-gather.11.cloned.1.call-done), kind=kOutput, calls=%fused_computation.5 | convolution fusion | flops 5943066624 | bytes 42467328 | tf_op jit(solution)/shard_map/dot_general | solution.py:34
  307.3 21.4 %multiply_reduce_fusion = (f32[1024]{0:T(1024)}, f32[1024]{0:T(1024)S(1)}, f32[1024,1024]{0,1:T(8,128)}) fusion(f32[1024,1024]{0,1:T(8,128)} %get-tuple-element.162, f32[1024]{0:T(1024)S(1)} %get-tuple-element.160, f32[1024]{0:T(1024)S(1)} %copy-done.29, bf16[1024,5632]{1,0:T(8,128)(2,1)} %all-gather.9.cloned.1.call-done, ...), kind=kOutput, calls=%fused_computation.32 | convolution fusion | flops 11840518144 | bytes 31473664 | tf_op jit(solution)/shard_map/dot_general | solution.py:34
  328.7 9.7 fusion.5
  338.4 2.1 copy-done.8
  340.5 3.8 convolution_convert_fusion.3
  344.3 11.1 %convolution_convert_fusion.2 = bf16[2816,1024]{1,0:T(8,128)(2,1)} fusion(bf16[1024,2816]{1,0:T(8,128)(2,1)} %multiply_convert_fusion.2, bf16[1024,1024]{0,1:T(8,128)(2,1)} %get-tuple-element.163), kind=kOutput, calls=%fused_computation.21 | convolution fusion | flops 5908463616 | bytes 13631488 | tf_op jit(solution)/shard_map/dot_general | solution.py:35
  355.5 20.0 %convolution_convert_fusion.1 = bf16[1024,5632]{1,0:T(8,128)(2,1)} fusion(bf16[1024,2816]{1,0:T(8,128)(2,1)} %get-tuple-element.138, bf16[1024,2816]{1,0:T(8,128)(2,1)} %get-tuple-element.137, f32[1024,1024]{0,1:T(8,128)} %get-tuple-element.162, f32[1024]{0:T(1024)S(1)} %copy-done.29, f32[1024]{0:T(1024)S(1)} %get-tuple-element.160), kind=kOutput, calls=%fused_computation.10 | convolution fusion | flops 11843141632 | bytes 27271168 | tf_op jit(solution)/shard_map/dot_general | solution.py:35
  375.6 7.3 fusion.18.gm_ref
  383.0 105.0 %mixer_bwd.1 = (bf16[1024,6144]{1,0:T(8,128)(2,1)}, f32[1024,256]{1,0:T(8,128)S(1)}, f32[16,32,128]{2,1,0:T(8,128)S(1)}, f32[4,8,5120]{2,1,0:T(8,128)S(1)}, f32[2,8,128]{2,1,0:T(8,128)S(1)}) custom-call(f32[1024,6272]{1,0:T(8,128)} %fusion.48.x_ref.xp_ref, f32[1024,6272]{1,0:T(8,128)} %fusion.48.x_ref.xp_ref, f32[4,5120]{1,0:T(4,128)S(1)} %bitcast.119, ...), custom_call_target="tpu_custom_call" | custom-call | tf_op jit(solution)/shard_map/mixer_bwd/pallas_call | solution.py:315
  488.0 1.3 copy.262
  489.3 1.7 fusion.51
  492.5 0.7 fusion.52
  493.3 1.0 reshape.222
  494.5 0.9 reshape.211
  495.4 1.0 copy.242
  496.4 2.4 broadcast_add_fusion
  498.8 1.3 copy.245
  500.2 0.9 copy.265
  501.6 0.8 convolution_convert_fusion.4
  502.4 20.5 %convolution_convert_fusion = bf16[1024,6144]{1,0:T(8,128)(2,1)} fusion(bf16[1024,6144]{1,0:T(8,128)(2,1)} %get-tuple-element.33, bf16[1024,1024]{0,1:T(8,128)(2,1)S(1)} %copy-done.7, f32[1024]{0:T(1024)S(1)} %copy-done.26, f32[1024]{0:T(1024)S(1)} %copy-done.24), kind=kOutput, calls=%fused_computation.9 | convolution fusion | flops 12895387648 | bytes 27271168 | tf_op jit(solution)/shard_map/dot_general | solution.py:35
  522.9 10.3 %pad_maximum_fusion = bf16[1024,6272]{1,0:T(8,128)(2,1)} fusion(bf16[1024,128]{1,0:T(8,128)(2,1)S(1)} %convolution_convert_fusion.4, bf16[1024,6144]{1,0:T(8,128)(2,1)} %convolution_convert_fusion), kind=kLoop, calls=%fused_computation | loop fusion | flops 25690112 | bytes 25690112 | tf_op jit(solution)/shard_map/concatenate | solution.py:496
  534.0 100.2 %reduce-scatter.5.cloned.1.call-done = bf16[256,6272]{1,0:T(8,128)(2,1)} async-done(((bf16[1024,6272]{1,0:T(8,128)(2,1)}), bf16[256,6272]{1,0:T(8,128)(2,1)}) %reduce-scatter.5.cloned.1.call-update) | async-done | bytes 3211280 | tf_op jit(solution)/shard_map/reduce_scatter | solution.py:402
  634.3 178.3 %all-reduce.9.cloned.1.call-done = (bf16[704,1024]{1,0:T(8,128)(2,1)}, bf16[256,5632]{1,0:T(8,128)(2,1)}, bf16[256,1024]{1,0:T(8,128)(2,1)}) async-done(((bf16[704,1024]{1,0:T(8,128)(2,1)}, bf16[256,5632]{1,0:T(8,128)(2,1)}, bf16[256,1024]{1,0:T(8,128)(2,1)}), (bf16[704,1024]{1,0:T(8,128)(2,1)}, bf16[256,5632]{1,0:T(8,128)(2,1)}, bf16[256,1024]{1,0:T(8,128)(2,1)})) %all-reduce.9.cloned.1.call-update) | async-done | bytes 4849680 | tf_op jit(solution)/shard_map/psum | solution.py:488
  812.6 19.5 %fusion = f32[1024,1024]{0,1:T(8,128)} fusion(bf16[1024,6144]{1,0:T(8,128)(2,1)} %get-tuple-element.33, bf16[1024,6272]{0,1:T(8,128)(2,1)} %all-gather.5.cloned.1.call-done), kind=kOutput, calls=%fused_computation.1 | convolution fusion | flops 12884901888 | bytes 29360128 | tf_op jit(solution)/shard_map/dot_general | solution.py:34
  832.5 5.7 fusion.14
  838.2 0.7 concatenate.34
  838.9 1.3 collective-permute-done
  840.2 1.5 collective-permute-start.1
  841.7 3.3 collective-permute-done.1
  845.0 1.5 collective-permute-start.2
  846.6 3.1 collective-permute-done.2
  849.8 9.8 %collective-permute-done.3 = f32[178,128]{1,0:T(8,128)S(1)} collective-permute-done((f32[178,128]{1,0:T(8,128)S(1)}, f32[178,128]{1,0:T(8,128)S(1)}, u32[]{:S(2)}, u32[]{:S(2)}) %collective-permute-start.3) | collective-permute-done | bytes 91168 | tf_op jit(solution)/shard_map/ppermute | solution.py:392
  859.7 5.9 fusion.13
  865.7 4.1 copy.253
  869.8 2.5 copy.254
  876.6 1.1 convert_element_type.88
  877.7 5.2 convert_element_type.89
  882.9 1.9 convert_element_type.90
  884.8 63.9 %all-reduce.7.cloned.1.call-done = bf16[256,6272]{1,0:T(8,128)(2,1)} async-done(((bf16[256,6272]{1,0:T(8,128)(2,1)}), bf16[256,6272]{1,0:T(8,128)(2,1)}) %all-reduce.7.cloned.1.call-update) | async-done | bytes 3211280 | tf_op jit(solution)/shard_map/psum | solution.py:503
  948.7 5.3 slice.134
  954.0 6.6 copy.251
  960.6 5.8 copy.252
  966.4 6.6 copy.255
  973.0 0.8 slice.135
  973.8 0.7 copy.256
  (166 shorter events, 14.8 us)
Async XLA Ops:
  7.2 94.0 %all-gather.5.cloned.1.call-start = ((), (), s32[]{:S(2)}) async-start(), calls=%async_computation.4 | async-start | bytes 16056320 | tf_op jit(solution)/shard_map/all_gather | solution.py:398
  10.4 0.7 copy-start.28
  13.0 2.1 copy-start.11
  13.0 220.6 %all-gather.7.cloned.1.call-start = ((), (), s32[]{:S(2)}) async-start(), calls=%async_computation.5 | async-start | bytes 2621440 | tf_op jit(solution)/shard_map/all_gather | solution.py:398
  13.8 226.7 %all-gather.9.cloned.1.call-start = ((), (), s32[]{:S(2)}) async-start(), calls=%async_computation.6 | async-start | bytes 14417920 | tf_op jit(solution)/shard_map/all_gather | solution.py:398
  14.5 258.7 %all-gather.11.cloned.1.call-start = ((), (), s32[]{:S(2)}) async-start(), calls=%async_computation.7 | async-start | bytes 7208960 | tf_op jit(solution)/shard_map/all_gather | solution.py:398
  15.1 518.2 %reduce-scatter.11.cloned.1.call-start = ((), (), s32[]{:S(2)}) async-start(), calls=%async_computation.11 | async-start | bytes 2621440 | tf_op jit(solution)/shard_map/reduce_scatter | solution.py:402
  21.6 5.1 copy-start.22
  21.7 5.3 copy-start.35
  21.7 79.5 %copy-start.25 = (f32[1024]{0:T(1024)S(1)}, f32[1024]{0:T(1024)}, u32[]{:S(2)}) copy-start(f32[1024]{0:T(1024)} %param.19) | copy-start | bytes 12292
  25.4 98.3 %copy-start.6 = (bf16[1024,1024]{0,1:T(8,128)(2,1)}, bf16[1024,1024]{0,1:T(8,128)(2,1)S(1)}, u32[]{:S(2)}) copy-start(bf16[1024,1024]{0,1:T(8,128)(2,1)S(1)} %copy.218) | copy-start | bytes 6291460
  26.7 74.5 %copy-start.23 = (f32[1024]{0:T(1024)}, f32[1024]{0:T(1024)S(1)}, u32[]{:S(2)}) copy-start(f32[1024]{0:T(1024)S(1)} %get-tuple-element.158) | copy-start | bytes 12292
  26.9 115.0 %copy-start.2 = (f32[1,4,2,2560]{3,1,2,0:T(4,128)}, f32[1,4,2,2560]{3,1,2,0:T(4,128)S(1)}, u32[]{:S(2)}) copy-start(f32[1,4,2,2560]{3,1,2,0:T(4,128)S(1)} %copy.269) | copy-start | bytes 245764
  26.9 101.3 %copy-start.33 = (f32[8]{0:T(128)}, f32[8]{0:T(128)S(1)}, u32[]{:S(2)}) copy-start(f32[8]{0:T(128)S(1)} %exponential_negate_fusion) | copy-start | bytes 100
  123.8 4.5 copy-start.31
  126.3 0.6 copy-start.15
  126.4 14.7 %copy-start.13 = (f32[16,64,2,8]{1,0,3,2:T(8,128)}, f32[16,64,2,8]{1,0,3,2:T(8,128)S(1)}, u32[]{:S(2)}) copy-start(f32[16,64,2,8]{1,0,3,2:T(8,128)S(1)} %reshape.203) | copy-start | bytes 196612
  128.2 0.6 copy-start.18
  137.4 4.6 copy-start.4
  233.0 0.7 copy-start
  233.6 6.9 copy-start.29
  307.3 21.4 %copy-start.9 = (bf16[1024,1024]{0,1:T(8,128)(2,1)S(1)}, bf16[1024,1024]{0,1:T(8,128)(2,1)}, u32[]{:S(2)}) copy-start(bf16[1024,1024]{0,1:T(8,128)(2,1)} %copy.233) | copy-start | bytes 6291460
  338.4 2.1 copy-start.8
  344.3 189.1 %reduce-scatter.7.cloned.1.call-start = ((), (), s32[]{:S(2)}) async-start(), calls=%async_computation.9 | async-start | bytes 7208960 | tf_op jit(solution)/shard_map/reduce_scatter | solution.py:402
  355.5 177.9 %reduce-scatter.9.cloned.1.call-start = ((), (), s32[]{:S(2)}) async-start(), calls=%async_computation.10 | async-start | bytes 14417920 | tf_op jit(solution)/shard_map/reduce_scatter | solution.py:402
  375.5 7.4 copy-start.1
  375.6 7.4 copy-start.3
  375.6 7.4 copy-start.5
  375.6 258.7 %reduce-scatter.5.cloned.1.call-start = ((), (), s32[]{:S(2)}) async-start(), calls=%async_computation.8 | async-start | bytes 16056320 | tf_op jit(solution)/shard_map/reduce_scatter | solution.py:402
  382.9 111.3 %copy-start.14 = (f32[16,64,2,8]{1,0,3,2:T(8,128)S(1)}, f32[16,64,2,8]{1,0,3,2:T(8,128)}, u32[]{:S(2)}) copy-start(f32[16,64,2,8]{1,0,3,2:T(8,128)} %copy-done.13) | copy-start | bytes 196612
  487.9 13.3 %copy-start.19 = (f32[1024,8]{0,1:T(8,128)S(1)}, f32[1024,8]{0,1:T(8,128)}, u32[]{:S(2)}) copy-start(f32[1024,8]{0,1:T(8,128)} %copy-done.18) | copy-start | bytes 98308
  487.9 13.3 %copy-start.32 = (f32[8]{0:T(128)S(1)}, f32[8]{0:T(128)}, u32[]{:S(2)}) copy-start(f32[8]{0:T(128)} %param.24) | copy-start | bytes 100
  488.0 13.3 %copy-start.34 = (f32[8]{0:T(128)S(1)}, f32[8]{0:T(128)}, u32[]{:S(2)}) copy-start(f32[8]{0:T(128)} %copy-done.33) | copy-start | bytes 100
  488.0 13.6 %copy-start.16 = (f32[1024,16]{0,1:T(8,128)S(1)}, f32[1024,16]{0,1:T(8,128)}, u32[]{:S(2)}) copy-start(f32[1024,16]{0,1:T(8,128)} %copy-done.15) | copy-start | bytes 196612
  488.0 13.6 %copy-start.24 = (f32[1024]{0:T(1024)S(1)}, f32[1024]{0:T(1024)}, u32[]{:S(2)}) copy-start(f32[1024]{0:T(1024)} %copy-done.23) | copy-start | bytes 12292
  488.0 13.6 %copy-start.26 = (f32[1024]{0:T(1024)S(1)}, f32[1024]{0:T(1024)}, u32[]{:S(2)}) copy-start(f32[1024]{0:T(1024)} %param.19) | copy-start | bytes 12292
  489.3 12.3 %copy-start.7 = (bf16[1024,1024]{0,1:T(8,128)(2,1)S(1)}, bf16[1024,1024]{0,1:T(8,128)(2,1)}, u32[]{:S(2)}) copy-start(bf16[1024,1024]{0,1:T(8,128)(2,1)} %copy-done.6) | copy-start | bytes 6291460
  493.2 8.4 copy-start.20
  493.2 8.4 copy-start.21
  533.3 279.3 %all-reduce.9.cloned.1.call-start = ((), (), s32[]{:S(2)}) async-start(), calls=%async_computation.13 | async-start | bytes 9699328 | tf_op jit(solution)/shard_map/psum | solution.py:488
  534.0 414.7 %all-reduce.7.cloned.1.call-start = ((), (), s32[]{:S(2)}) async-start(), calls=%async_computation.12 | async-start | bytes 6422528 | tf_op jit(solution)/shard_map/psum | solution.py:503
  832.4 5.7 copy-start.30
  832.4 27.3 %copy-start.27 = (f32[1024]{0:T(1024)S(1)}, f32[1024]{0:T(1024)}, u32[]{:S(2)}) copy-start(f32[1024]{0:T(1024)} %get-tuple-element.157) | copy-start | bytes 12292
  838.9 1.3 collective-permute-start
  840.2 4.8 collective-permute-start.1
  845.0 4.6 collective-permute-start.2
  849.7 9.9 %collective-permute-start.3 = (f32[178,128]{1,0:T(8,128)S(1)}, f32[178,128]{1,0:T(8,128)S(1)}, u32[]{:S(2)}, u32[]{:S(2)}) collective-permute-start(f32[178,128]{1,0:T(8,128)S(1)} %add.149), channel_id=1, source_target_pairs={{0,8},{1,9},{2,10},{3,11},{4,12},{5,13},{6,14},{7,15},{8,0},{9,1},... | collective-permute-start | bytes 273416 | tf_op jit(solution)/shard_map/ppermute | solution.py:392
  859.7 12.7 %collective-permute-start.4 = (f32[178,128]{1,0:T(8,128)S(1)}, f32[178,128]{1,0:T(8,128)S(1)}, u32[]{:S(2)}, u32[]{:S(2)}) collective-permute-start(f32[178,128]{1,0:T(8,128)S(1)} %add.150), channel_id=1, source_target_pairs={{0,16},{1,17},{2,18},{3,19},{4,20},{5,21},{6,22},{7,23},{8,24},{9,... | collective-permute-start | bytes 273416 | tf_op jit(solution)/shard_map/ppermute | solution.py:392
  865.7 4.1 copy-start.10
  865.7 11.0 %copy-start.17 = (bf16[256,1024]{1,0:T(8,128)(2,1)S(1)}, bf16[256,1024]{1,0:T(8,128)(2,1)}, u32[]{:S(2)}) copy-start(bf16[256,1024]{1,0:T(8,128)(2,1)} %get-tuple-element.39) | copy-start | bytes 1572868
  877.7 5.2 copy-start.12
Sparse Core Ops, SparseCore 0:
  13.2 87.9 all-gather.4
  102.8 22.5 all-gather.6
  126.9 76.1 all-gather.8
  204.5 43.3 all-gather.10
  344.4 31.5 reduce-scatter.10
  378.6 54.8 reduce-scatter.6
  436.0 92.1 reduce-scatter.8
  533.4 100.8 reduce-scatter.4
  638.2 174.2 all-reduce.8
  816.5 132.1 all-reduce.6

commit v2 on v1

v2 whole, which is shorter than its diff:
```python
import functools

import jax
import jax.numpy as jnp
from jax import lax
from jax.experimental import pallas as pl
from jax.experimental.pallas import tpu as pltpu
from jax.sharding import PartitionSpec as P

HEADS = 8
DK = 128
HOUSE = 2
BLOCK = 64
EPSILON = 1e-06
EPS = EPSILON
f32 = jnp.float32
bf16 = jnp.bfloat16


def dot_plain(a,b): return nn(a,b)
def dot_right_t(a,b): return nt(a,b)
def dot_left_t(a,b): return tn(a,b)
def nn(a,b): return lax.dot_general(a,b,(((1,),(0,)),((),())),preferred_element_type=f32)
def nt(a,b): return lax.dot_general(a,b,(((1,),(1,)),((),())),preferred_element_type=f32)
def tn(a,b): return lax.dot_general(a,b,(((0,),(0,)),((),())),preferred_element_type=f32)
def lo(x): return x.astype(bf16)
def sigmoid(x): return 0.5*jnp.tanh(0.5*x)+0.5
def cat(*xs): return jnp.concatenate(xs,axis=0)

def token_masks(C):
    row=lax.broadcasted_iota(jnp.int32,(C,2*C),0)
    col=lax.broadcasted_iota(jnp.int32,(C,2*C),1)
    left=col<C
    tok=jnp.where(left,col,col-C)
    return row,tok,left

LU=2
PREC=lax.Precision.HIGHEST

def exact(a,b,dims): return lax.dot_general(a,b,(dims,((),())),precision=PREC,preferred_element_type=f32)

def col6(slot,h):
    at=(h//LU)*6*LU*128+slot*LU*128+(h%LU)*128
    return slice(at,at+128)

def col5(slot,h):
    at=(h//LU)*5*LU*128+slot*LU*128+(h%LU)*128
    return slice(at,at+128)

def coln(slot,h):
    at=slot*HEADS*DK+h*DK
    return slice(at,at+DK)

def gates(colg,rowg,h):
    return colg[:,16+h:17+h],rowg[8+h:9+h,:],rowg[h:h+1,:]

def softplus(v): return jnp.maximum(v,0.0)+jnp.log1p(jnp.exp(-jnp.abs(v)))

def eyes(C):
    row,tok,left=token_masks(C)
    here=tok==row
    return jnp.where(here&left,1.0,0.0),jnp.where(here&jnp.logical_not(left),1.0,0.0),jnp.where(row<=tok,1.0,0.0)

def square_mask(C,upper):
    a=lax.broadcasted_iota(jnp.int32,(C,C),0)
    b=lax.broadcasted_iota(jnp.int32,(C,C),1)
    return jnp.where((b>=a) if upper else (b<=a),1.0,0.0)

def gate_body(C,NB,sm_ref,par_ref,col_ref,row_ref):
    eyeL,eyeR,tri2=eyes(C)
    tri=square_mask(C,False)
    lane=lax.broadcasted_iota(jnp.int32,(C,128),1)
    for b in range(NB):
        sl=slice(b*C,b*C+C)
        sm=sm_ref[sl,:]
        beta=sigmoid(sm)
        g=par_ref[0:1,:]*softplus(sm+par_ref[1:2,:])
        c=exact(tri,g,((1,),(0,)))
        col_ref[sl,:]=jnp.where(lane<16,beta,c)
        crow=exact(g,tri2,((0,),(0,)))
        brow=exact(beta,eyeL,((0,),(0,)))[0:8]+exact(beta,eyeR,((0,),(0,)))[8:16]
        row_ref[b,0:8,:]=brow
        row_ref[b,8:16,:]=crow[16:24]

def gate_fwd(small,par,C,NB=4,at=0):
    R=small.shape[0]; NC=R//C
    return pl.pallas_call(
        functools.partial(gate_body,C,NB),grid=(NC//NB,),
        in_specs=[pl.BlockSpec((NB*C,128),lambda n:(n,at)),pl.BlockSpec((8,128),lambda n:(0,0))],
        out_specs=[pl.BlockSpec((NB*C,128),lambda n:(n,0)),pl.BlockSpec((NB,16,128),lambda n:(n,0,0))],
        out_shape=[jax.ShapeDtypeStruct((R,128),f32),jax.ShapeDtypeStruct((NC,16,128),f32)],
        name="gate_fwd")(small,par)

def gate_bwd_body(C,NB,K,*refs):
    sm_ref,par_ref,colg_ref=refs[:3]
    cols=refs[3:3+K]; rows=refs[3+K:3+2*K]
    out_ref,acc_ref=refs[3+2*K:]
    @pl.when(pl.program_id(0)==0)
    def _():
        acc_ref[...]=jnp.zeros_like(acc_ref)
    eyeL,eyeR,tri2=eyes(C)
    tru=square_mask(C,True)
    lane=lax.broadcasted_iota(jnp.int32,(C,128),1)
    z=lambda n: jnp.zeros((n,128),f32)
    part=lambda v: jnp.sum(v.reshape(C//8,8,128),axis=0)
    for b in range(NB):
        sl=slice(b*C,b*C+C)
        col=cols[0][sl,:]; row=rows[0][b]
        for k in range(1,K):
            col=col+cols[k][sl,:]; row=row+rows[k][b]
        cs=row[0:8]; dss=row[8:16]
        ccs=exact(eyeL,cat(cs,z(120)),((1,),(1,)))+exact(eyeR,cat(z(8),cs,z(112)),((1,),(1,)))
        beta=jnp.where(lane<16,colg_ref[sl,:],0.0)
        d=jnp.where(lane<16,col,0.0)
        dbeta=ccs+d
        y=beta*dbeta
        dc=col-pltpu.roll(y,16,1)-pltpu.roll(y,8,1)
        bd=jnp.sum(beta*d,axis=0,keepdims=True)
        bd=cat(bd,z(7))
        dcl=exact(jnp.ones((8,128),f32),cat(z(16),dss,z(104)),((1,),(1,)))[0:1]+(pltpu.roll(bd,16,1)+pltpu.roll(bd,8,1))[0:1]
        keep=(lane>=16)&(lane<24)
        dc=jnp.where(keep,dc,0.0)
        dg=exact(tru,dc,((1,),(0,)))+dcl
        dg=jnp.where(keep,dg,0.0)
        pre=sm_ref[sl,:]+par_ref[1:2,:]
        g=par_ref[0:1,:]*softplus(pre)
        dpre=dg*par_ref[0:1,:]*sigmoid(pre)
        out_ref[sl,:]=lo(jnp.where(lane<16,dbeta*beta*(1.0-beta),dpre))
        acc_ref[0:8,:]+=part(dpre)
        acc_ref[8:16,:]+=part(dg*g)

def gate_bwd(small,par,colg,cols,rows,C,NB=4,at=0):
    R=small.shape[0]; NC=R//C; K=len(cols)
    cspec=pl.BlockSpec((NB*C,128),lambda n:(n,0)); rspec=pl.BlockSpec((NB,16,128),lambda n:(n,0,0))
    return pl.pallas_call(
        functools.partial(gate_bwd_body,C,NB,K),grid=(NC//NB,),
        in_specs=[pl.BlockSpec((NB*C,128),lambda n:(n,at)),pl.BlockSpec((8,128),lambda n:(0,0)),cspec]+[cspec]*K+[rspec]*K,
        out_specs=[cspec,pl.BlockSpec((16,128),lambda n:(0,0))],
        out_shape=[jax.ShapeDtypeStruct((R,128),bf16),jax.ShapeDtypeStruct((16,128),f32)],
        name="gate_bwd")(small,par,colg,*cols,*rows)

def fwd_body(C,HB,NB,hoff,x_ref,cw_ref,colg_ref,rowg_ref,nh_ref,*refs):
    mixed_ref,o_ref,s0_ref,t_ref,u_ref,xs,S=refs[-7:]
    fwd_main(C,HB,NB,hoff,x_ref,cw_ref,colg_ref,rowg_ref,nh_ref,mixed_ref,o_ref,s0_ref,t_ref,u_ref,xs,S)

def fwd_main(C,HB,NB,hoff,x_ref,cw_ref,colg_ref,rowg_ref,nh_ref,mixed_ref,o_ref,s0_ref,t_ref,u_ref,xs,S):
    NR=NB*C
    nu=HB//LU
    @pl.when(pl.program_id(1)==0)
    def _():
        xs[0:8,:]=jnp.zeros((8,xs.shape[1]),f32)
        S[...]=jnp.zeros_like(S)
    @pl.when(pl.program_id(1)!=0)
    def _():
        xs[0:8,:]=xs[NR:NR+8,:]
    for u in range(nu):
        w5=5*LU*128
        xs[8:8+NR,u*w5:(u+1)*w5]=x_ref[:,u*6*LU*128:u*6*LU*128+w5].astype(f32)
    row,tok,left=token_masks(C)
    incl=tok<=row
    strict=tok<row
    botm=tok<row+jnp.where(left,1,0)
    eye=jnp.where((tok==row)&left,1.0,0.0)
    eye2=jnp.where((tok==row)&jnp.logical_not(left),1.0,0.0)
    def act(slot,b,h):
        sl=col5(slot,h)
        cn=coln(slot,hoff+h)
        y=cw_ref[3:4,cn]*xs[8+b*C:8+b*C+C,sl]
        for i in range(3):
            y=y+cw_ref[i:i+1,cn]*xs[5+i+b*C:5+i+b*C+C,sl]
        return y*sigmoid(y)
    def l2(a): return a*lax.rsqrt(jnp.sum(a*a,axis=-1,keepdims=True)+EPS)
    H=[(b,h) for b in range(NB) for h in range(HB)]
    colg=[colg_ref[b*C:b*C+C,:] for b in range(NB)]
    rowg=[rowg_ref[b] for b in range(NB)]
    Q={};K={};V={};Y={};Kb={};GP={};A={};M={};T={}
    for p in H:
        b,h=p
        Q[p]=l2(act(0,b,h))*(128**-0.5)
        K[p]=cat(l2(act(1,b,h)),l2(act(2,b,h)))
        V[p]=cat(act(3,b,h),act(4,b,h))
        Y[p]=lo(cat(Q[p],K[p]))
        Kb[p]=lo(K[p])
    for p in H:
        GP[p]=nt(Y[p],Kb[p])
    for p in H:
        b,h=p
        c_col,c_row,b_row=gates(colg[b],rowg[b],hoff+h)
        e=jnp.exp(jnp.minimum(c_col-c_row,0.0))*b_row
        M[p]=lo(jnp.where(incl,GP[p][0:C]*e,0.0))
        A[p]=cat(jnp.where(strict,GP[p][C:2*C]*e,0.0),jnp.where(botm,GP[p][2*C:3*C]*e,0.0))
        T[p]=cat(eye,eye2-A[p][C:2*C]*eye)
    s=1
    while s<C:
        m=((tok//(2*s))==(row//(2*s)))&((row//s)%2==1)&((tok//s)%2==0)
        mf=jnp.where(m,1.0,0.0)
        Tb={p:lo(T[p]) for p in H}
        Z={p:nn(lo(cat(A[p][0:C]*mf,A[p][C:2*C]*mf)),Tb[p]) for p in H}
        T={p:T[p]-nn(Tb[p],lo(Z[p])) for p in H}
        s*=2
    Tb={p:lo(T[p]) for p in H}
    for b in range(NB):
        S0=[S[:,h*128:h*128+128] for h in range(HB)]
        S0b=[lo(v) for v in S0]
        YS=[nn(Y[b,h],S0b[h]) for h in range(HB)]
        U=[]
        for h in range(HB):
            ec=jnp.exp(colg[b][:,16+hoff+h:17+hoff+h])
            ks=YS[h][C:3*C]
            R=V[b,h]-cat(ec*ks[0:C],ec*ks[C:2*C])
            U.append(lo(nn(Tb[b,h],lo(R))))
        for h in range(HB):
            sl=slice(h*128,h*128+128)
            G=hoff+h
            rows=slice(b*C,b*C+C)
            c_col=colg[b][:,16+G:17+G]
            ec=jnp.exp(c_col)
            cl=c_col[C-1:C]
            ew=jnp.exp(cl-c_col)
            w0=ew*colg[b][:,G:G+1]
            w1=ew*colg[b][:,8+G:9+G]
            kw=lo(cat(w0*K[b,h][0:C],w1*K[b,h][C:2*C]))
            S[:,sl]=jnp.exp(cl)*S0[h]+tn(kw,U[h])
            O=ec*YS[h][0:C]+nn(M[b,h],U[h])
            s0_ref[b,:,sl]=S0b[h]
            t_ref[b,:,sl]=Tb[b,h]
            u_ref[b,:,sl]=U[h]
            o_ref[rows,sl]=O
            g=x_ref[rows,col6(5,h)].astype(f32)
            r=lax.rsqrt(jnp.mean(O*O,axis=-1,keepdims=True)+EPS)
            mixed_ref[rows,sl]=lo(O*r*nh_ref[...]*(g*sigmoid(g)))

def mixer_fwd(x,cw,colg,rowg,nh,nseq,hoff,HB,C,NB=2,mixed=None):
    R=x.shape[0]; nch=R//nseq//C//NB; W=HB*128
    rb=lambda s,n:(s*nch+n,0)
    cb=lambda s,n:(s*nch+n,0,0)
    NC=R//C
    big=pl.BlockSpec((NB,128,W),cb)
    state=jax.ShapeDtypeStruct((NC,128,W),bf16)
    return pl.pallas_call(
        functools.partial(fwd_body,C,HB,NB,hoff),
        grid=(nseq,nch),
        in_specs=[pl.BlockSpec((NB*C,6*W),rb),pl.BlockSpec((4,5*HEADS*DK),lambda s,n:(0,0)),
                  pl.BlockSpec((NB*C,128),rb),pl.BlockSpec((NB,16,128),cb),
                  pl.BlockSpec((1,128),lambda s,n:(0,0))]+([pl.BlockSpec(memory_space=pl.ANY)] if mixed is not None else []),
        input_output_aliases={5:0} if mixed is not None else {},
        out_specs=[pl.BlockSpec((NB*C,W),lambda s,n:(s*nch+n,hoff//HB)),pl.BlockSpec((NB*C,W),rb),big,big,big],
        out_shape=[jax.ShapeDtypeStruct((R,HEADS*DK),bf16),jax.ShapeDtypeStruct((R,W),f32),state,state,state],
        scratch_shapes=[pltpu.VMEM((NB*C+8,5*W),f32),pltpu.VMEM((128,W),f32)],
        compiler_params=pltpu.CompilerParams(dimension_semantics=("arbitrary",)*2,vmem_limit_bytes=56<<20),
        cost_estimate=pl.CostEstimate(flops=HB*10_000_000_000,transcendentals=0,bytes_accessed=HB*30_000_000),
        name="mixer_fwd",
    )(x,cw,colg,rowg,nh,*(() if mixed is None else (mixed,)))

def bwd_body(C,HB,hoff,x_ref,xp_ref,cw_ref,colg_ref,rowg_ref,nh_ref,gm_ref,o_ref,s0_ref,t_ref,u_ref,
             gx_ref,col_ref,row_ref,dcw_ref,dnh_ref,xs,gs,dS):
    W=HB*128
    CV=5*W
    n=pl.program_id(1); nch=pl.num_programs(1)
    first=(pl.program_id(0)==0)&(n==0)
    @pl.when(first)
    def _():
        dcw_ref[...]=jnp.zeros_like(dcw_ref)
        dnh_ref[...]=jnp.zeros_like(dnh_ref)
    @pl.when(n==0)
    def _():
        gs[C:C+8,:]=jnp.zeros((8,CV),f32)
        dS[...]=jnp.zeros_like(dS)
    @pl.when(n!=0)
    def _():
        gs[C:C+8,:]=gs[0:8,:]
    @pl.when(n==nch-1)
    def _():
        xs[0:8,:]=jnp.zeros((8,CV),f32)
    w5=5*LU*128
    parts=[(slice(u*w5,(u+1)*w5),slice(u*6*LU*128,u*6*LU*128+w5)) for u in range(HB//LU)]
    @pl.when(n!=nch-1)
    def _():
        for to,at in parts:
            xs[0:8,to]=xp_ref[:,at].astype(f32)
    for to,at in parts:
        xs[8:8+C,to]=x_ref[:,at].astype(f32)
    row,tok,left=token_masks(C)
    incl=tok<=row
    strict=tok<row
    botm=tok<row+jnp.where(left,1,0)
    colg=colg_ref[...]
    rowg=rowg_ref[0]
    lane=lax.broadcasted_iota(jnp.int32,(C,128),1)
    H=range(HB)
    def conv(slot,h):
        sl=col5(slot,h)
        cn=coln(slot,hoff+h)
        y=cw_ref[3:4,cn]*xs[8:8+C,sl]
        for i in range(3):
            y=y+cw_ref[i:i+1,cn]*xs[5+i:5+i+C,sl]
        return y
    def act_norm(slot,h):
        y=conv(slot,h)
        sg=sigmoid(y)
        a=y*sg
        r=lax.rsqrt(jnp.sum(a*a,axis=-1,keepdims=True)+EPS)
        dsil=sg*(1.0+y*(1.0-sg))
        return a*r,r,dsil
    Q=[];K=[];rq=[];rk0=[];rk1=[];dq_s=[];dk0_s=[];dk1_s=[]
    for h in H:
        a,r,d=act_norm(0,h); Q.append(a*(128**-0.5)); rq.append(r); dq_s.append(d)
        a0,r0,d0=act_norm(1,h); a1,r1,d1=act_norm(2,h)
        K.append(cat(a0,a1)); rk0.append(r0); rk1.append(r1); dk0_s.append(d0); dk1_s.append(d1)
    dO=[]
    nhg=nh_ref[...]
    for h in H:
        sl=slice(h*128,h*128+128)
        O=o_ref[:,sl]; gm=gm_ref[:,sl].astype(f32)
        gt=x_ref[:,col6(5,h)].astype(f32)
        sg=sigmoid(gt)
        r=lax.rsqrt(jnp.mean(O*O,axis=-1,keepdims=True)+EPS)
        on=O*r
        gsil=gm*(gt*sg)
        t1=gsil*on
        dnh_ref[0]+=jnp.sum(t1.reshape(C//8,8,128),axis=0)
        dgt=gm*(on*nhg)*(sg*(1.0+gt*(1.0-sg)))
        gx_ref[:,col6(5,h)]=lo(dgt)
        u=gsil*nhg
        dO.append(r*(u-on*jnp.mean(u*on,axis=-1,keepdims=True)))
    Y=[cat(Q[h],K[h]) for h in H]
    Yb=[lo(y) for y in Y]
    Kb=[lo(K[h]) for h in H]
    GP=[nt(Yb[h],Kb[h]) for h in H]
    dU=[];Eq=[];EA=[];dSb=[];ecs=[];ews=[]
    for h in H:
        sl=slice(h*128,h*128+128)
        c_col,c_row,b_row=gates(colg,rowg,hoff+h)
        e=jnp.exp(jnp.minimum(c_col-c_row,0.0))
        eq=jnp.where(incl,e,0.0); ea=cat(jnp.where(strict,e,0.0),jnp.where(botm,e,0.0))
        Eq.append(eq);EA.append(ea)
        M=lo(GP[h][0:C]*eq*b_row)
        cl=colg[C-1:C,16+hoff+h:17+hoff+h]
        ec=jnp.exp(c_col); ew=jnp.exp(cl-c_col)
        ecs.append(ec);ews.append(ew)
        w0=ew*colg[:,hoff+h:hoff+h+1]
        w1=ew*colg[:,8+hoff+h:9+hoff+h]
        kw=lo(cat(w0*K[h][0:C],w1*K[h][C:2*C]))
        db_=lo(dS[:,sl]); dSb.append(db_)
        dU.append(lo(tn(M,lo(dO[h]))+nn(kw,db_)))
    dR=[tn(t_ref[0,:,h*128:h*128+128],dU[h]) for h in H]
    dAM=[nt(lo(cat(dO[h],-dR[h])),u_ref[0,:,h*128:h*128+128]) for h in H]
    Z=[]
    for h in H:
        ec=ecs[h]
        Z.append(lo(cat(ec*dO[h],-(ec*dR[h][0:C]),-(ec*dR[h][C:2*C]))))
    UdS=[nt(u_ref[0,:,h*128:h*128+128],dSb[h]) for h in H]
    colout=jnp.zeros((C,128),f32)
    rows=[]
    X=[]
    ZS=[nt(Z[h],s0_ref[0,:,h*128:h*128+128]) for h in H]
    for h in H:
        sl=slice(h*128,h*128+128)
        cl=colg[C-1:C,16+hoff+h:17+hoff+h]
        b_row=rowg[hoff+h:hoff+h+1,:]
        S0f=s0_ref[0,:,sl].astype(f32)
        dSf=dS[:,sl]
        dSS=jnp.sum(dSf*S0f,axis=0,keepdims=True)*jnp.exp(cl)
        dS[:,sl]=jnp.exp(cl)*dSf+tn(Yb[h],Z[h])
        dM=dAM[h][0:C]; dA=dAM[h][C:3*C]
        xm=dM*Eq[h]; xa=dA*EA[h]
        XM=xm*GP[h][0:C]; XA=xa*GP[h][C:3*C]
        cs=jnp.sum(XM,axis=0,keepdims=True)+jnp.sum(XA,axis=0,keepdims=True)
        rows.append((cs,dSS))
        XMb=XM*b_row
        XAb=XA*b_row
        rs=jnp.sum(XMb+XAb[0:C]+XAb[C:2*C],axis=-1,keepdims=True)
        yz=Y[h]*ZS[h]
        rs=rs+jnp.sum(yz[0:C]+yz[C:2*C]+yz[2*C:3*C],axis=-1,keepdims=True)
        ku=K[h]*UdS[h]
        d0=ews[h]*jnp.sum(ku[0:C],axis=-1,keepdims=True)
        d1=ews[h]*jnp.sum(ku[C:2*C],axis=-1,keepdims=True)
        colout=jnp.where(lane==16+hoff+h,rs,colout)
        colout=jnp.where(lane==hoff+h,d0,colout)
        colout=jnp.where(lane==8+hoff+h,d1,colout)
        X.append(lo(cat(xm*b_row,xa[0:C]*b_row,xa[C:2*C]*b_row)))
    col_ref[...]=colout
    row_ref[...]=jnp.zeros_like(row_ref)
    for h in H:
        row_ref[0,hoff+h:hoff+h+1,:]=rows[h][0]
        row_ref[0,8+hoff+h:9+hoff+h,:]=rows[h][1]
    XK=[nn(X[h],Kb[h]) for h in H]
    XY=[tn(X[h],Yb[h]) for h in H]
    def l2b(g,nrm,r):
        return r*(g-nrm*jnp.sum(g*nrm,axis=-1,keepdims=True))
    for h in H:
        ew=ews[h]
        w0=ew*colg[:,hoff+h:hoff+h+1]
        w1=ew*colg[:,8+hoff+h:9+hoff+h]
        sl=lambda s: col5(s,h)
        dq=ZS[h][0:C]+XK[h][0:C]
        dk=ZS[h][C:3*C]+XK[h][C:3*C]+XY[h]
        dk0=dk[0:C]+w0*UdS[h][0:C]
        dk1=dk[C:2*C]+w1*UdS[h][C:2*C]
        gs[0:C,sl(0)]=l2b(dq*(128**-0.5),Q[h]*(128**0.5),rq[h])*dq_s[h]
        gs[0:C,sl(1)]=l2b(dk0,K[h][0:C],rk0[h])*dk0_s[h]
        gs[0:C,sl(2)]=l2b(dk1,K[h][C:2*C],rk1[h])*dk1_s[h]
        for j in range(2):
            y=conv(3+j,h); sg=sigmoid(y)
            gs[0:C,sl(3+j)]=dR[h][j*C:j*C+C]*(sg*(1.0+y*(1.0-sg)))
        for s in range(5):
            g=gs[0:C,sl(s)]
            cn=coln(s,hoff+h)
            gx=cw_ref[3:4,cn]*g
            dcw_ref[3,:,cn]+=jnp.sum((g*xs[8:8+C,sl(s)]).reshape(C//8,8,128),axis=0)
            for i in range(3):
                gx=gx+cw_ref[i:i+1,cn]*gs[3-i:3-i+C,sl(s)]
                dcw_ref[i,:,cn]+=jnp.sum((g*xs[5+i:5+i+C,sl(s)]).reshape(C//8,8,128),axis=0)
            gx_ref[:,col6(s,h)]=lo(gx)

def mixer_bwd(x,cw,colg,rowg,nh,gm,o,s0,t,u,nseq,hoff,unit,C,HB=2):
    R=x.shape[0]; nch=R//nseq//C; W=HB*128
    ch=lambda s,n: s*nch+nch-1-n
    rb=lambda s,n:(ch(s,n),unit)
    r0=lambda s,n:(ch(s,n),0)
    cb=lambda s,n:(ch(s,n),0,unit)
    NC=nseq*nch
    big=pl.BlockSpec((1,128,W),cb)
    return pl.pallas_call(
        functools.partial(bwd_body,C,HB,hoff),
        grid=(nseq,nch),
        in_specs=[pl.BlockSpec((C,6*W),rb),
                  pl.BlockSpec((8,6*W),lambda s,n:(jnp.maximum(ch(s,n)*(C//8)-1,0),unit)),
                  pl.BlockSpec((4,5*HEADS*DK),lambda s,n:(0,0)),
                  pl.BlockSpec((C,128),r0),pl.BlockSpec((1,16,128),lambda s,n:(ch(s,n),0,0)),
                  pl.BlockSpec((1,128),lambda s,n:(0,0)),
                  pl.BlockSpec((C,W),lambda s,n:(ch(s,n),hoff//HB)),pl.BlockSpec((C,W),rb),
                  big,big,big],
        out_specs=[pl.BlockSpec((C,6*W),r0),pl.BlockSpec((C,128),r0),
                   pl.BlockSpec((1,16,128),lambda s,n:(ch(s,n),0,0)),
                   pl.BlockSpec((4,8,5*HEADS*DK),lambda s,n:(0,0,0)),
                   pl.BlockSpec((1,8,128),lambda s,n:(0,0,0))],
        out_shape=[jax.ShapeDtypeStruct((R,6*W),bf16),jax.ShapeDtypeStruct((R,128),f32),
                   jax.ShapeDtypeStruct((NC,16,128),f32),
                   jax.ShapeDtypeStruct((4,8,5*HEADS*DK),f32),jax.ShapeDtypeStruct((1,8,128),f32)],
        scratch_shapes=[pltpu.VMEM((C+8,5*W),f32),pltpu.VMEM((C+8,5*W),f32),pltpu.VMEM((128,W),f32)],
        compiler_params=pltpu.CompilerParams(dimension_semantics=("arbitrary",)*2,vmem_limit_bytes=48<<20),
        cost_estimate=pl.CostEstimate(flops=100_000_000,transcendentals=0,bytes_accessed=300_000),
        name="mixer_bwd",
    )(x,x,cw,colg,rowg,nh,gm,o,s0,t,u)


def sort_body(w_ref, small_ref, out_ref, first_ref, second_ref):
    width = LU * DK
    for unit in range(4):
        for slot in range(6):
            at = slot * HEADS * DK + unit * width
            to = (unit % 2) * 6 * width + slot * width
            dst = (first_ref, second_ref)[unit // 2]
            dst[:, to : to + width] = w_ref[:, at : at + width]
    first_ref[:, 12 * width :] = small_ref[...]
    second_ref[:, 12 * width :] = out_ref[...]


def sort_weights(w_in, w_small, w_out):
    rows = w_in.shape[0]
    wide = 12 * LU * DK
    return pl.pallas_call(
        sort_body,
        out_shape=[
            jax.ShapeDtypeStruct((rows, wide + DK), bf16),
            jax.ShapeDtypeStruct((rows, wide + w_out.shape[1]), bf16),
        ],
        compiler_params=pltpu.CompilerParams(vmem_limit_bytes=48 << 20),
        name="sort_weights",
    )(w_in, w_small, w_out)


def natural_columns(parts):
    width = LU * DK
    count = parts[0].shape[1] // width
    return jnp.concatenate(
        [p[:, j * width : (j + 1) * width] for j in range(count) for p in parts], axis=1
    )


def all_sum(vec, total):
    axes = ("rep", "shard")
    step = 1
    while step < total:
        vec = vec + lax.ppermute(vec, axes, [(i, i ^ step) for i in range(total)])
        step *= 2
    return vec


def swap(x, axis, count, bit):
    return lax.ppermute(x, axis, [(i, i ^ bit) for i in range(count)])


def pick(blocks, index):
    return lax.dynamic_index_in_dim(blocks, index, 0, keepdims=False)


def tie(x, *deps):
    return lax.optimization_barrier((x,) + deps)[0]


def scatter(grad):
    return lax.psum_scatter(grad, "shard", scatter_dimension=0, tiled=True)


def gather(w):
    return lax.all_gather(w, "shard", axis=0, tiled=True)


def pair_body(added, idx_ref, a_ref, b_ref, g_ref, *refs):
    ins, outs = refs[: 2 * added], refs[2 * added :]
    g = g_ref[...]
    for k, lhs in enumerate((a_ref, b_ref)):
        out = tn(lhs[...], g)
        if added:
            out = out + ins[k][...].astype(f32)
        outs[k][...] = lo(out)


def grad_pair(lhs, g, idx, added=()):
    rows, wide = lhs.shape
    block = wide // 4
    cols = g.shape[1]
    tile = 512 if cols % 512 == 0 else 256
    out = jax.ShapeDtypeStruct((block, cols), bf16)
    flat = pl.BlockSpec((block, tile), lambda j, idx: (0, j))
    return pl.pallas_call(
        functools.partial(pair_body, len(added) // 2),
        grid_spec=pltpu.PrefetchScalarGridSpec(
            num_scalar_prefetch=1,
            grid=(cols // tile,),
            in_specs=[
                pl.BlockSpec((rows, block), lambda j, idx: (0, idx[0])),
                pl.BlockSpec((rows, block), lambda j, idx: (0, idx[1])),
                pl.BlockSpec((rows, tile), lambda j, idx: (0, j)),
            ]
            + [flat] * len(added),
            out_specs=[flat, flat],
        ),
        out_shape=[out, out],
        compiler_params=pltpu.CompilerParams(vmem_limit_bytes=48 << 20),
        cost_estimate=pl.CostEstimate(
            flops=100_000_000, transcendentals=0, bytes_accessed=300_000
        ),
        name="grad_pair",
    )(idx, lhs, lhs, g, *added)


def ends(me, bits):
    return jnp.stack([me ^ b for b in bits]).astype(jnp.int32)


def project_body(idx_ref, *refs):
    lhs, rhs, out = refs[:4], refs[4:8], refs[8]
    total = nn(lhs[0][...], rhs[0][...])
    for a, b in zip(lhs[1:], rhs[1:]):
        total = total + nn(a[...], b[...])
    out[...] = total


def project(x, pieces):
    me = lax.axis_index("shard")
    rows, wide = x.shape
    block, cols = pieces[0].shape
    tile = 640
    pick_lhs = lambda p: pl.BlockSpec((rows, block), lambda j, idx: (0, idx[p]))
    return pl.pallas_call(
        project_body,
        grid_spec=pltpu.PrefetchScalarGridSpec(
            num_scalar_prefetch=1,
            grid=(cols // tile,),
            in_specs=[pick_lhs(p) for p in range(4)]
            + [pl.BlockSpec((block, tile), lambda j, idx: (0, j))] * 4,
            out_specs=pl.BlockSpec((rows, tile), lambda j, idx: (0, j)),
        ),
        out_shape=jax.ShapeDtypeStruct((rows, cols), f32),
        compiler_params=pltpu.CompilerParams(vmem_limit_bytes=48 << 20),
        name="project",
    )(ends(me, (0, 1, 2, 3)), x, x, x, x, *pieces)


def pull_first_body(idx_ref, g_ref, small_ref, *refs):
    pieces, out = refs[:4], refs[4]
    block, cols = pieces[0].shape
    wide = g_ref.shape[1]
    for p in range(4):
        w = pieces[p]
        part = nt(g_ref[...], w[:, 0:wide]) + nt(small_ref[...], w[:, wide:cols])
        out[:, pl.ds(pl.multiple_of(idx_ref[p] * block, block), block)] = part


def pull_first(g, small, pieces):
    me = lax.axis_index("shard")
    rows, wide = g.shape
    tile = 256
    whole = pl.BlockSpec(pieces[0].shape, lambda i, idx: (0, 0), pipeline_mode=pl.Buffered(1))
    width = 4 * pieces[0].shape[0]
    return pl.pallas_call(
        pull_first_body,
        grid_spec=pltpu.PrefetchScalarGridSpec(
            num_scalar_prefetch=1,
            grid=(rows // tile,),
            in_specs=[
                pl.BlockSpec((tile, wide), lambda i, idx: (i, 0)),
                pl.BlockSpec((tile, small.shape[1]), lambda i, idx: (i, 0)),
            ]
            + [whole] * 4,
            out_specs=pl.BlockSpec((tile, width), lambda i, idx: (i, 0)),
        ),
        out_shape=jax.ShapeDtypeStruct((rows, width), f32),
        compiler_params=pltpu.CompilerParams(vmem_limit_bytes=48 << 20),
        name="pull_first",
    )(ends(me, (0, 1, 2, 3)), g, small, *pieces)


def pull_second_body(count, *refs):
    gs, (w_ref, part_ref, h_ref, res_ref, gain_ref, out_ref, acc_ref) = refs[:count], refs[count:]
    grad = part_ref[...]
    at = 0
    for g in gs:
        wide = g.shape[1]
        grad = grad + nt(g[...], w_ref[:, at : at + wide])
        at += wide
    h = h_ref[...].astype(f32)
    r = lax.rsqrt(jnp.mean(h * h, axis=-1, keepdims=True) + EPS)
    u = grad * gain_ref[...]
    back = r * u - (r * r * r) * h * jnp.mean(u * h, axis=-1, keepdims=True)
    out_ref[...] = lo(res_ref[...] + back)

    @pl.when(pl.program_id(0) == 0)
    def _():
        acc_ref[...] = jnp.zeros_like(acc_ref)

    t = grad * h * r
    acc_ref[...] += jnp.sum(t.reshape(t.shape[0] // 8, 8, t.shape[1]), axis=0)


def pull_second(gs, w, part, hidden, residual, gain):
    rows, width = hidden.shape
    tile = 256
    wide = sum(g.shape[1] for g in gs)
    row = lambda cols: pl.BlockSpec((tile, cols), lambda i: (i, 0))
    return pl.pallas_call(
        functools.partial(pull_second_body, len(gs)),
        grid=(rows // tile,),
        in_specs=[row(g.shape[1]) for g in gs]
        + [
            pl.BlockSpec((w.shape[0], wide), lambda i: (0, 0), pipeline_mode=pl.Buffered(1)),
            row(width),
            row(width),
            row(width),
            pl.BlockSpec((1, width), lambda i: (0, 0)),
        ],
        out_specs=[row(width), pl.BlockSpec((8, width), lambda i: (0, 0))],
        out_shape=[
            jax.ShapeDtypeStruct((rows, width), bf16),
            jax.ShapeDtypeStruct((8, width), f32),
        ],
        compiler_params=pltpu.CompilerParams(vmem_limit_bytes=56 << 20),
        name="pull_second",
    )(*gs, w, part, hidden, residual, gain.reshape(1, width))


def first_half(lhs, g):
    me = lax.axis_index("shard")
    near, far = grad_pair(lhs, g, ends(me, (1, 3)))
    return near, swap(near, "shard", 4, 1), swap(far, "shard", 4, 1)


def second_half(lhs, g, got):
    me = lax.axis_index("shard")
    part, own = grad_pair(lhs, g, ends(me, (2, 0)), (got[1], got[0]))
    return part, own, swap(part, "shard", 4, 2)


def rep_stages(own, across, late):
    rows, cols = own.shape
    me = lax.axis_index("rep")
    low = me & 1
    high = me >> 1
    own2 = own.reshape(2, rows // 2, cols)
    across2 = tie(across, late[0]).reshape(2, rows // 2, cols)
    both = lambda i: pick(own2, i).astype(f32) + pick(across2, i).astype(f32)
    send = lo(both(1 - low))
    other = swap(send, "rep", 8, 1)
    yield send
    other = tie(other, late[0])
    half = lo(both(low) + other.astype(f32)).reshape(4, rows // 8, cols)
    cuts = [pick(half, high ^ d) for d in (1, 2, 3)]
    got = [swap(c, "rep", 8, 2 * d) for c, d in zip(cuts, (1, 2, 3))]
    yield half
    got[0] = tie(got[0], late[0])
    piece = pick(half, high).astype(f32)
    for v in got:
        piece = piece + v.astype(f32)
    piece = lo(piece)
    pieces = [swap(piece, "rep", 8, 2 * d) for d in (1, 2, 3)]
    yield piece
    pieces = jnp.stack([piece, tie(pieces[0], late[0])] + pieces[1:])
    half = jnp.concatenate([pick(pieces, high ^ k) for k in range(4)], axis=0)
    other = swap(half, "rep", 8, 1)
    yield half
    both2 = jnp.stack([half, tie(other, late[0])])
    yield jnp.concatenate([pick(both2, low), pick(both2, low ^ 1)], axis=0)


def shards(
    rep_count,
    shard_count,
    hidden_in,
    teacher,
    cotangent,
    lengths,
    norm_attn,
    w_in,
    w_small,
    conv_w,
    a_log,
    dt_bias,
    norm_head,
    w_out,
    norm_mlp,
    w_mlp_in,
    w_mlp_down,
):
    row_count, width = hidden_in.shape
    seq_here = lengths.shape[0]
    slot_count = row_count // seq_here
    small_width = w_small.shape[1]
    total = rep_count * shard_count
    plain = shard_count == 4 and rep_count == 8
    unit_width = 6 * LU * DK
    part_width = 2 * unit_width
    w_small_pad = jnp.pad(w_small, ((0, 0), (0, 128 - small_width)))
    first, second = sort_weights(w_in, w_small_pad, w_out)
    if plain:
        crossed = swap(first, "shard", 4, 2)
        near = swap(first, "shard", 4, 1)
        pieces = (first, near, crossed, swap(crossed, "shard", 4, 1))
    else:
        w_first = gather(first)
    second_all = gather(second)
    w_second = second_all[:, :part_width]
    w_out_all = second_all[:, part_width:]
    w_mlp_in_all = gather(w_mlp_in)
    w_down_all = gather(w_mlp_down)

    hidden32 = hidden_in.astype(f32)
    r_in = lax.rsqrt(jnp.mean(hidden32 * hidden32, axis=-1, keepdims=True) + EPSILON)
    normed_low = (hidden32 * r_in * norm_attn).astype(bf16)
    if plain:
        proj_first = project(normed_low, pieces)
    else:
        proj_first = dot_plain(normed_low, w_first)
    head_gain = norm_head.reshape(1, DK)
    pad_lanes = ((16, 104),)
    decay_par = jnp.concatenate(
        [
            jnp.pad(-jnp.exp(a_log), pad_lanes).reshape(1, 128),
            jnp.pad(dt_bias, pad_lanes).reshape(1, 128),
            jnp.zeros((6, 128), f32),
        ],
        axis=0,
    )
    gate_at = part_width // 128
    colg, rowg = gate_fwd(proj_first, decay_par, BLOCK, at=gate_at)
    kept_first = mixer_fwd(proj_first, conv_w, colg, rowg, head_gain, seq_here, 0, 4, BLOCK, 4)
    proj_second = dot_plain(tie(normed_low, kept_first[0]), w_second)
    kept_second = mixer_fwd(
        proj_second, conv_w, colg, rowg, head_gain, seq_here, 4, 4, BLOCK, 4, kept_first[0]
    )
    mixed_low = kept_second[0]
    residual = hidden32 + dot_plain(mixed_low, w_out_all)
    r_mid = lax.rsqrt(jnp.mean(residual * residual, axis=-1, keepdims=True) + EPSILON)
    mid_low = (residual * r_mid * norm_mlp).astype(bf16)
    gate_up = dot_plain(mid_low, w_mlp_in_all)
    unit_count = w_down_all.shape[0]
    gate_part = gate_up[:, :unit_count]
    up_part = gate_up[:, unit_count:]
    sigmoid_gate = jax.nn.sigmoid(gate_part)
    silu_gate = gate_part * sigmoid_gate
    product_low = (silu_gate * up_part).astype(bf16)
    output32 = residual + dot_plain(product_low, w_down_all)
    slot_index = lax.broadcasted_iota(jnp.int32, (seq_here, slot_count), 1)
    valid_rows = (slot_index < lengths[:, None]).astype(f32).reshape(row_count, 1)
    deviation = output32 - teacher.astype(f32)
    loss_sum = jnp.sum(valid_rows * deviation * deviation)
    valid_count = jnp.sum(lengths).astype(f32)
    grad_out = valid_rows * (cotangent.astype(f32) + deviation)
    grad_out_low = grad_out.astype(bf16)

    grad_w_down = dot_left_t(product_low, grad_out_low).astype(bf16)
    own_down = scatter(grad_w_down)
    grad_product = dot_right_t(tie(grad_out_low, grad_w_down), w_down_all)
    grad_gate = grad_product * up_part * sigmoid_gate * (1.0 + gate_part * (1.0 - sigmoid_gate))
    grad_up = grad_product * silu_gate
    grad_gate_up = jnp.concatenate([grad_gate, grad_up], axis=1).astype(bf16)
    if plain:
        mlp_near, *mlp_got = first_half(mid_low, grad_gate_up)
        grad_mid = dot_right_t(tie(grad_gate_up, mlp_near), w_mlp_in_all)
        mlp_part, mlp_own, mlp_across = second_half(
            mid_low, tie(grad_gate_up, grad_mid), mlp_got
        )
        grad_mid, own_down = lax.optimization_barrier((tie(grad_mid, mlp_part), own_down))
        own_down = lax.psum(own_down, "rep")
    else:
        grad_w_mlp_in = dot_left_t(mid_low, grad_gate_up).astype(bf16)
        own_mlp_in = scatter(grad_w_mlp_in)
        grad_mid = dot_right_t(tie(grad_gate_up, grad_w_mlp_in), w_mlp_in_all)
    u_mid = grad_mid * norm_mlp
    grad_norm_mlp = jnp.sum(grad_mid * residual * r_mid, axis=0)
    grad_residual = (
        grad_out
        + r_mid * u_mid
        - (r_mid * r_mid * r_mid) * residual * jnp.mean(u_mid * residual, axis=-1, keepdims=True)
    )
    grad_res_low = grad_residual.astype(bf16)
    grad_mixed = dot_right_t(grad_res_low, w_out_all)
    if plain:
        out_near, *out_got = first_half(mixed_low, tie(grad_res_low, grad_mixed))
        deps = [out_near]
    else:
        grad_w_out = dot_left_t(mixed_low, grad_res_low).astype(bf16)
        own_out = scatter(grad_w_out)
        deps = [grad_w_out]

    projs = (proj_first, proj_second)
    kept = (kept_first, kept_second)
    pulled = []
    running = {}
    finals = {}

    late = [None]

    def advance(keys, dep):
        late[0] = dep
        outs = []
        for key in keys:
            value = next(running[key], None)
            if value is not None:
                finals[key] = value
                outs.append(value)
        return outs

    for index, (head, count) in enumerate(((0, 4), (4, 2), (6, 2))):
        half = head // 4
        if index == 1 and plain:
            own_mlp_in = lo(mlp_own.astype(f32) + tie(mlp_across, *deps).astype(f32))
            own_mlp_in, own_down = lax.optimization_barrier((own_mlp_in, own_down))
            deps = deps + [own_mlp_in]
            own_mlp_in = lax.psum(own_mlp_in, "rep")
        back = mixer_bwd(
            projs[half], conv_w, colg, rowg, head_gain, tie(grad_mixed, *deps),
            *kept[half][1:], seq_here, head, (head % 4) // count, BLOCK, count,
        )
        pulled.append(back)
        gx = back[0]
        if not plain:
            grad = dot_left_t(normed_low, gx).astype(bf16)
            finals[index] = lax.psum(scatter(grad), "rep")
            deps = [grad]
            continue
        if index == 0:
            gx = tie(gx, own_down)
        near, *got = first_half(normed_low, gx)
        outs = [near]
        if index == 0:
            out_part, out_own, out_across = second_half(
                mixed_low, tie(grad_res_low, near), out_got
            )
            outs.append(out_part)
        if index == 2:
            outs += advance([0], near)
        part, own, across = second_half(normed_low, tie(gx, *outs), got)
        if index == 0:
            own = jnp.concatenate([own, out_own], axis=1)
            across = jnp.concatenate([across, out_across], axis=1)
        running[index] = rep_stages(own, across, late)
        deps = [part]
    if not plain:
        own_down, own_mlp_in, own_out = lax.psum((own_down, own_mlp_in, own_out), "rep")
    cols = tuple(p[1] for p in pulled)
    rows = tuple(p[2] for p in pulled)
    col_last = tie(cols[-1], own_mlp_in, *deps)
    grad_small_low, gate_sums = gate_bwd(
        proj_first, decay_par, colg, cols[:-1] + (col_last,), rows, BLOCK, at=gate_at
    )
    grad_w_small = dot_left_t(grad_small_low, normed_low)[:small_width]
    gxs = [p[0] for p in pulled]

    def checkpoint(value, keys):
        if not plain:
            return value
        return tie(value, *advance(keys, value))

    gx_zero = checkpoint(tie(gxs[0], grad_small_low), [0, 1])
    if plain:
        grad_part = pull_first(gx_zero, grad_small_low, pieces)
    else:
        grad_part = dot_right_t(gx_zero, w_first[:, :part_width]) + dot_right_t(
            grad_small_low, w_first[:, part_width:]
        )
    gx_one = checkpoint(tie(gxs[1], grad_part), [0, 1, 2])
    grad_hidden, attn_part = pull_second(
        (gx_one, gxs[2]), second_all, grad_part, hidden_in, grad_residual, norm_attn
    )
    grad_norm_attn = checkpoint(jnp.sum(attn_part, axis=0), [0, 1, 2])
    grad_conv = sum(jnp.sum(p[3], axis=1) for p in pulled)
    grad_gain = sum(jnp.sum(p[4], axis=(0, 1)) for p in pulled)
    parts = (
        grad_conv.reshape(-1),
        grad_w_small.reshape(-1),
        grad_norm_mlp,
        grad_gain,
        jnp.sum(gate_sums[8:, 16:24], axis=0),
        jnp.sum(gate_sums[:8, 16:24], axis=0),
        loss_sum.reshape(1),
        valid_count.reshape(1),
        jnp.zeros((110,), f32),
    )
    packed = jnp.concatenate(parts).reshape(-1, 128)
    packed = all_sum(packed, total).reshape(-1)
    sums = []
    start = 0
    for part in parts:
        sums.append(packed[start : start + part.shape[0]])
        start += part.shape[0]
    sum_attn = all_sum(grad_norm_attn.reshape(-1, 128), total).reshape(-1)
    own_rows = w_small.shape[0]
    own_small = lax.dynamic_slice_in_dim(
        sums[1].reshape(small_width, width), lax.axis_index("shard") * own_rows, own_rows, 1
    )
    loss_value = sums[6][0] / (sums[7][0] * width)
    if plain:
        late[0] = grad_norm_attn
        for key in (0, 1, 2):
            for value in running[key]:
                finals[key] = value
        own_out = finals[0][:, part_width:]
    units = [finals[0][:, :unit_width], finals[0][:, unit_width:part_width], finals[1], finals[2]]
    return (
        output32.astype(bf16),
        loss_value,
        grad_hidden,
        sum_attn,
        natural_columns(units).astype(f32),
        own_small.T,
        sums[0].reshape(conv_w.shape),
        sums[4],
        sums[5],
        sums[3],
        own_out.astype(f32),
        sums[2],
        own_mlp_in.astype(f32),
        own_down.astype(f32),
    )


def solution(mesh):
    in_specs = (
        P(("rep", "shard"), None),
        P(("rep", "shard"), None),
        P(("rep", "shard"), None),
        P(("rep", "shard")),
        P(),
        P("shard", None),
        P("shard", None),
        P(),
        P(),
        P(),
        P(),
        P("shard", None),
        P(),
        P("shard", None),
        P("shard", None),
    )
    out_specs = (
        P(("rep", "shard"), None),
        P(),
        P(("rep", "shard"), None),
        P(),
        P("shard", None),
        P("shard", None),
        P(),
        P(),
        P(),
        P(),
        P("shard", None),
        P(),
        P("shard", None),
        P("shard", None),
    )
    return jax.shard_map(
        functools.partial(shards, mesh.shape["rep"], mesh.shape["shard"]),
        mesh=mesh,
        in_specs=in_specs,
        out_specs=out_specs,
        check_vma=False,
    )
```

time: 992 us -> 776 us (0.78)
  waiting for transfers between devices: 437 us -> 172 us
  Pallas kernels: 196 us -> 292 us
  matrix products: 195 us -> 107 us
  starting transfers between devices: 3.61 us -> 61.3 us
  local copies, waits for them, and re-layouts: 70.7 us -> 22.9 us
  other arithmetic: 62.9 us -> 90.9 us
    psum x2, waiting for transfers between devices: 242 us -> 34.2 us  [the longest x1 23.9 us: shards(): own_mlp_in = lax.psum(own_mlp_in, 'rep')]
    ppermute x0 -> x42, waiting for transfers between devices: none -> 110 us  [swap(): return lax.ppermute(x, axis, [(i, i ^ bit) for i in range(count)])]
    reduce_scatter x4 -> x1, waiting for transfers between devices: 100 us -> 0.01 us  [scatter(): return lax.psum_scatter(grad, 'shard', scatter_dimension=0, tiled=True)]
    pallas_call x2 -> x21, Pallas kernels: 196 us -> 292 us  [the longest x3 111 us: mixer_bwd(): pl.pallas_call(functools.partial(bwd_body, C, HB, hoff), grid=(nseq, nch)...]
    all_gather x4 -> x3, waiting for transfers between devices: 74.2 us -> 12.2 us  [gather(): return lax.all_gather(w, 'shard', axis=0, tiled=True)]
    ppermute x0 -> x42, starting transfers between devices: none -> 50.8 us  [swap(): return lax.ppermute(x, axis, [(i, i ^ bit) for i in range(count)])]
    dot_general x5 -> x2, matrix products: 56.1 us -> 8.51 us  [tn(): lax.dot_general(a, b, (((0,), (0,)), ((), ())), preferred_element_type=f32)]
    dot_general x5 -> x3, matrix products: 74.5 us -> 47.8 us  [nt(): lax.dot_general(a, b, (((1,), (1,)), ((), ())), preferred_element_type=f32)]
  transfers between devices with their start and end apart: 15 -> 58, of which waited for: 8 -> 22; matrix products, arithmetic and copies ran while one was open for 23% -> 23% of each run, Pallas kernels for 20% -> 38%
where the time goes in v2:
time: 776 us; the launch traced here: 765 us
  Pallas kernels  292 us (38%)
  waiting for transfers between devices  172 us (22%)
  matrix products  107 us (14%)
  other arithmetic  90.9 us (12%)
  starting transfers between devices  61.3 us (8%)
  local copies, waits for them, and re-layouts  22.9 us (3%)
  between operations  19 us (2%)
    pallas_call x3, Pallas kernels, mixer_bwd(): pl.pallas_call(functools.partial(bwd_body, C, HB, hoff), grid=(nseq, nch)...  111 us
    ppermute x42, waiting for transfers between devices, swap(): return lax.ppermute(x, axis, [(i, i ^ bit) for i in range(count)])  110 us
    pallas_call x10, Pallas kernels, grad_pair(): pl.pallas_call(functools.partial(pair_body, len(added) // 2), grid_spec=p...  71.7 us
    pallas_call x2, Pallas kernels, mixer_fwd(): pl.pallas_call(functools.partial(fwd_body, C, HB, NB, hoff), grid=(nseq,...  54.4 us
    ppermute x42, starting transfers between devices, swap(): return lax.ppermute(x, axis, [(i, i ^ bit) for i in range(count)])  50.8 us
    dot_general x4, matrix products, nn(): lax.dot_general(a, b, (((1,), (0,)), ((), ())), preferred_element_type=f32)  50.2 us
    dot_general x3, matrix products, nt(): lax.dot_general(a, b, (((1,), (1,)), ((), ())), preferred_element_type=f32)  47.8 us
    psum x1, waiting for transfers between devices, shards(): own_mlp_in = lax.psum(own_mlp_in, 'rep')  23.9 us
  transfers between devices with their start and end apart: 58, of which 22 were waited for; matrix products, arithmetic and copies ran while one was open for 23% of the time, Pallas kernels for 38%

profile of v2, /device:TPU:0, one launch (start us, length us, event | category | flops | bytes accessed | tf_op | source)
XLA Modules:
  0.0 764.8 jit_solution(4050619916917761035)
XLA Ops:
  9.1 2.3 sort_weights.1
  13.6 3.0 collective-permute-start.1
  16.6 62.7 %collective-permute-done.1.refs_6_.refs_2_ = bf16[256,3200]{1,0:T(8,128)(2,1)S(1)} collective-permute-done((bf16[256,3200]{1,0:T(8,128)(2,1)S(1)}, bf16[256,3200]{1,0:T(8,128)(2,1)S(1)}, u32[]{:S(2)}, u32[]{:S(2)}) %collective-permute-start.1) | collective-permute-done | bytes 1638432 | tf_op jit(solution)/shard_map/ppermute | solution.py:492
  81.7 2.1 fusion.3
  85.7 13.5 %project.1.sm_ref.x_ref.xp_ref.refs_0_ = f32[1024,3200]{1,0:T(8,128)} custom-call(s32[4]{0:T(128)S(1)} %pad_add_fusion.idx_ref, bf16[1024,1024]{1,0:T(8,128)(2,1)} %fusion.5.refs_0_.refs_1_.refs_2_.refs_3_.a_ref.b_ref, bf16[1024,1024]{1,0:T(8,128)(2,1)} %fusion.5.refs_0_.refs_1_.refs_2_.refs_3_.a_ref.b_ref, ...), custom_call_target="tpu_custom_call" | custom-call | tf_op jit(solution)/shard_map/project/pallas_call | solution.py:568
  99.2 5.3 gate_fwd.1
  104.5 26.7 %mixer_fwd.2 = (bf16[1024,1024]{1,0:T(8,128)(2,1)}, f32[1024,512]{1,0:T(8,128)}, bf16[16,128,512]{2,1,0:T(8,128)(2,1)}, bf16[16,128,512]{2,1,0:T(8,128)(2,1)}, bf16[16,128,512]{2,1,0:T(8,128)(2,1)}) custom-call(f32[1024,3200]{1,0:T(8,128)} %project.1.sm_ref.x_ref.xp_ref.refs_0_, f32[4,5120]{1,0:T(4,128)} %cw_ref.9, ...), custom_call_target="tpu_custom_call" | custom-call | flops 40000000000 | bytes 120000000 | tf_op jit(solution)/shard_map/mixer_fwd/pallas_call | solution.py:240
  131.2 12.3 %fusion.1.x_ref.xp_ref = f32[1024,3072]{1,0:T(8,128)} fusion(bf16[1024,1024]{1,0:T(8,128)(2,1)S(1)} %copy-done, bf16[1024,4096]{1,0:T(8,128)(2,1)} %all-gather.4.cloned.1.call-done.refs_2_), kind=kOutput, calls=%fused_computation.6 | convolution fusion | flops 6442450944 | bytes 20971520 | tf_op jit(solution)/shard_map/dot_general | solution.py:23
  143.5 27.7 %mixer_fwd.3 = (bf16[1024,1024]{1,0:T(8,128)(2,1)}, f32[1024,512]{1,0:T(8,128)}, bf16[16,128,512]{2,1,0:T(8,128)(2,1)}, bf16[16,128,512]{2,1,0:T(8,128)(2,1)}, bf16[16,128,512]{2,1,0:T(8,128)(2,1)}) custom-call(f32[1024,3072]{1,0:T(8,128)} %fusion.1.x_ref.xp_ref, f32[4,5120]{1,0:T(4,128)} %cw_ref.9, ...), custom_call_target="tpu_custom_call", output_to_operand_aliasing={{0}: (5, {})} | custom-call | flops 40000000000 | bytes 120000000 | tf_op jit(solution)/shard_map/mixer_fwd/pallas_call | solution.py:240
  171.2 4.7 multiply_reduce_fusion.2
  179.6 20.0 %fusion.69 = f32[1024,5632]{1,0:T(8,128)} fusion(bf16[1024,1024]{1,0:T(8,128)(2,1)} %multiply_convert_fusion.3.a_ref.b_ref, bf16[1024,5632]{1,0:T(8,128)(2,1)} %all-gather.6.cloned.1.call-done), kind=kOutput, calls=%fused_computation.196 | convolution fusion | flops 11811160064 | bytes 36700160 | tf_op jit(solution)/shard_map/dot_general | solution.py:23
  199.6 11.6 %multiply_convert_fusion.2 = bf16[1024,2816]{1,0:T(8,128)(2,1)} fusion(f32[1024,5632]{1,0:T(8,128)} %fusion.69), kind=kLoop, calls=%fused_computation.3 | loop fusion | flops 17301504 | bytes 28835840 | tf_op jit(solution)/shard_map/convert_element_type | solution.py:783
  211.2 12.1 %all-gather.8.cloned.1.call-done = bf16[2816,1024]{1,0:T(8,128)(2,1)} async-done(((bf16[704,1024]{1,0:T(8,128)(2,1)}), bf16[2816,1024]{1,0:T(8,128)(2,1)}) %all-gather.8.cloned.1.call-update) | async-done | bytes 5767184 | tf_op jit(solution)/shard_map/all_gather | solution.py:508
  223.4 13.2 %fusion.32 = (bf16[1024,1024]{1,0:T(8,128)(2,1)S(1)}, f32[1024,1024]{1,0:T(8,128)}) fusion(bf16[1024,1024]{1,0:T(8,128)(2,1)} %param.16, bf16[1024,1024]{1,0:T(8,128)(2,1)} %param.17, f32[1024]{0:T(1024)S(1)} %copy-done.64, f32[1024,1024]{1,0:T(8,128)} %copy-done.48, bf16[1024,2816]{1,0:T(8,128)(2,1)} %multiply_convert_fusion.2, ...), kind=kOutput, calls=%fused_computation.100 | convolution fusion | flops 5912920064 | bytes 26218496 | tf_op jit(solution)/shard_map/dot_general | solution.py:23
  237.9 8.1 %convolution_convert_fusion = bf16[2816,1024]{1,0:T(8,128)(2,1)} fusion(bf16[1024,2816]{1,0:T(8,128)(2,1)S(1)} %copy-done.53, bf16[1024,1024]{1,0:T(8,128)(2,1)S(1)} %get-tuple-element.114), kind=kOutput, calls=%fused_computation.13 | convolution fusion | flops 5908463616 | bytes 13631488 | tf_op jit(solution)/shard_map/dot_general | solution.py:25
  246.2 22.3 %multiply_convert_fusion.1 = (bf16[1024,2816]{1,0:T(8,128)(2,1)}, bf16[1024,2816]{1,0:T(8,128)(2,1)}) fusion(f32[1024,5632]{1,0:T(8,128)} %fusion.69, bf16[1024,1024]{1,0:T(8,128)(2,1)} %copy-done.70, bf16[2816,1024]{1,0:T(8,128)(2,1)} %all-gather.8.cloned.1.call-done), kind=kOutput, calls=%fused_computation.2 | convolution fusion | flops 5943066624 | bytes 42467328 | tf_op jit(solution)/shard_map/dot_general | solution.py:24
  268.5 10.2 %pad_maximum_fusion.g_ref = bf16[1024,5632]{1,0:T(8,128)(2,1)} fusion(bf16[1024,2816]{1,0:T(8,128)(2,1)} %get-tuple-element.207, bf16[1024,2816]{1,0:T(8,128)(2,1)} %get-tuple-element.206), kind=kLoop, calls=%fused_computation | loop fusion | flops 23068672 | bytes 23068672 | tf_op jit(solution)/shard_map/concatenate | solution.py:798
  278.7 13.8 %grad_pair.10 = (bf16[256,5632]{1,0:T(8,128)(2,1)S(1)}, bf16[256,5632]{1,0:T(8,128)(2,1)}) custom-call(s32[2]{0:T(128)S(1)} %pad_add_fusion.1.idx_ref, bf16[1024,1024]{1,0:T(8,128)(2,1)S(1)} %copy-done.2, bf16[1024,1024]{1,0:T(8,128)(2,1)S(1)} %copy-done.2, bf16[1024,5632]{1,0:T(8,128)(2,1)} %pad_maximum_fusion.g_ref), custom_call_target="tpu_custom_call" | custom-call | flops 100000000 | bytes 300000 | tf_op jit(solution)/shard_map/grad_pair/pallas_call | solution.py:528
  293.0 18.7 %fusion.70 = f32[1024,1024]{1,0:T(8,128)} fusion(bf16[1024,5632]{1,0:T(8,128)(2,1)} %pad_maximum_fusion.g_ref, bf16[1024,5632]{1,0:T(8,128)(2,1)} %all-gather.6.cloned.1.call-done), kind=kOutput, calls=%fused_computation.197 | convolution fusion | flops 11811160064 | bytes 27262976 | tf_op jit(solution)/shard_map/dot_general | solution.py:24
  314.9 14.8 %grad_pair.11 = (bf16[256,5632]{1,0:T(8,128)(2,1)}, bf16[256,5632]{1,0:T(8,128)(2,1)}) custom-call(s32[2]{0:T(128)S(1)} %pad_add_fusion.2.idx_ref, bf16[1024,1024]{1,0:T(8,128)(2,1)S(1)} %copy-done.2, bf16[1024,1024]{1,0:T(8,128)(2,1)S(1)} %copy-done.2, bf16[1024,5632]{1,0:T(8,128)(2,1)} %pad_maximum_fusion.g_ref, bf16[256,5632]{1,0:T(8,128)(2,1)} %copy-done.55, ...), custom_call_target="tpu_custom_call" | custom-call | flops 100000000 | bytes 300000 | tf_op jit(solution)/shard_map/grad_pair/pallas_call | solution.py:528
  329.8 5.1 multiply_reduce_fusion
  335.0 11.2 %fusion.66 = (bf16[1024,1024]{1,0:T(8,128)(2,1)S(1)}, f32[1024,1024]{1,0:T(8,128)}, f32[]{:T(128)}, bf16[1024,1024]{1,0:T(8,128)(2,1)}) fusion(f32[1024]{0:T(1024)S(1)} %broadcast_multiply_fusion, f32[1024,1024]{1,0:T(8,128)} %copy-done.48, f32[1024]{0:T(1024)S(1)} %copy-done.63, f32[1024,1024]{1,0:T(8,128)} %fusion.70, f32[1024]{0:T(1024)S(1)} %copy-done.61, ...), kind=kLoop, calls=%fused_computation.193 | loop fusion | flops 16777215 | bytes 25186308 | tf_op jit(solution)/shard_map/convert_element_type | solution.py:818
  346.2 6.8 fusion.8.gm_ref
  353.0 2.4 grad_pair.12
  356.3 53.8 %mixer_bwd.3 = (bf16[1024,3072]{1,0:T(8,128)(2,1)}, f32[1024,128]{1,0:T(8,128)S(1)}, f32[16,16,128]{2,1,0:T(8,128)S(1)}, f32[4,8,5120]{2,1,0:T(8,128)S(1)}, f32[1,8,128]{2,1,0:T(8,128)S(1)}) custom-call(f32[1024,3200]{1,0:T(8,128)} %project.1.sm_ref.x_ref.xp_ref.refs_0_, f32[1024,3200]{1,0:T(8,128)} %project.1.sm_ref.x_ref.xp_ref.refs_0_, ...), custom_call_target="tpu_custom_call" | custom-call | flops 100000000 | bytes 300000 | tf_op jit(solution)/shard_map/mixer_bwd/pallas_call | solution.py:424
  412.4 10.3 %all-reduce.6.cloned.1.call-done = bf16[704,1024]{1,0:T(8,128)(2,1)} async-done(((bf16[704,1024]{1,0:T(8,128)(2,1)}), bf16[704,1024]{1,0:T(8,128)(2,1)}) %all-reduce.6.cloned.1.call-update) | async-done | bytes 1441808 | tf_op jit(solution)/shard_map/psum | solution.py:806
  422.7 7.7 %grad_pair.13 = (bf16[256,3072]{1,0:T(8,128)(2,1)S(1)}, bf16[256,3072]{1,0:T(8,128)(2,1)S(1)}) custom-call(s32[2]{0:T(128)S(1)} %pad_add_fusion.1.idx_ref, bf16[1024,1024]{1,0:T(8,128)(2,1)S(1)} %copy-done, bf16[1024,1024]{1,0:T(8,128)(2,1)S(1)} %copy-done, bf16[1024,3072]{1,0:T(8,128)(2,1)} %get-tuple-element.180.g_ref), custom_call_target="tpu_custom_call" | custom-call | flops 100000000 | bytes 300000 | tf_op jit(solution)/shard_map/grad_pair/pallas_call | solution.py:528
  431.5 5.4 collective-permute-done.5.refs_0_
  437.7 3.4 grad_pair.14
  442.2 8.5 %grad_pair.15 = (bf16[256,3072]{1,0:T(8,128)(2,1)}, bf16[256,3072]{1,0:T(8,128)(2,1)S(1)}) custom-call(s32[2]{0:T(128)S(1)} %pad_add_fusion.2.idx_ref, bf16[1024,1024]{1,0:T(8,128)(2,1)} %fusion.5.refs_0_.refs_1_.refs_2_.refs_3_.a_ref.b_ref, bf16[1024,1024]{1,0:T(8,128)(2,1)} %fusion.5.refs_0_.refs_1_.refs_2_.refs_3_.a_ref.b_ref, ...), custom_call_target="tpu_custom_call" | custom-call | flops 100000000 | bytes 300000 | tf_op jit(solution)/shard_map/grad_pair/pallas_call | solution.py:528
  453.4 4.1 add_convert_fusion
  459.1 28.5 %mixer_bwd.4 = (bf16[1024,1536]{1,0:T(8,128)(2,1)}, f32[1024,128]{1,0:T(8,128)S(1)}, f32[16,16,128]{2,1,0:T(8,128)S(1)}, f32[4,8,5120]{2,1,0:T(8,128)S(1)}, f32[1,8,128]{2,1,0:T(8,128)S(1)}) custom-call(f32[1024,3072]{1,0:T(8,128)} %fusion.1.x_ref.xp_ref, f32[1024,3072]{1,0:T(8,128)} %fusion.1.x_ref.xp_ref, f32[4,5120]{1,0:T(4,128)S(1)} %copy-done.23, ...), custom_call_target="tpu_custom_call" | custom-call | flops 100000000 | bytes 300000 | tf_op jit(solution)/shard_map/mixer_bwd/pallas_call | solution.py:424
  487.7 5.5 grad_pair.16
  497.0 5.1 grad_pair.17
  503.0 28.4 %mixer_bwd.5 = (bf16[1024,1536]{1,0:T(8,128)(2,1)}, f32[1024,128]{1,0:T(8,128)S(1)}, f32[16,16,128]{2,1,0:T(8,128)S(1)}, f32[4,8,5120]{2,1,0:T(8,128)S(1)}, f32[1,8,128]{2,1,0:T(8,128)S(1)}) custom-call(f32[1024,3072]{1,0:T(8,128)} %fusion.1.x_ref.xp_ref, f32[1024,3072]{1,0:T(8,128)} %fusion.1.x_ref.xp_ref, f32[4,5120]{1,0:T(4,128)S(1)} %copy-done.24, ...), custom_call_target="tpu_custom_call" | custom-call | flops 100000000 | bytes 300000 | tf_op jit(solution)/shard_map/mixer_bwd/pallas_call | solution.py:424
  531.5 5.3 grad_pair.18
  544.7 2.0 reduce_sum.134
  546.8 3.3 convert_element_type.267
  553.1 5.1 grad_pair.19
  559.8 23.9 %all-reduce.8.cloned.1.call-done = bf16[256,5632]{1,0:T(8,128)(2,1)} async-done(((bf16[256,5632]{1,0:T(8,128)(2,1)}), bf16[256,5632]{1,0:T(8,128)(2,1)}) %all-reduce.8.cloned.1.call-update) | async-done | bytes 2883600 | tf_op jit(solution)/shard_map/psum | solution.py:852
  583.6 8.1 %gate_bwd.1 = (bf16[1024,128]{1,0:T(8,128)(2,1)}, f32[16,128]{1,0:T(8,128)}) custom-call(f32[1024,3200]{1,0:T(8,128)} %project.1.sm_ref.x_ref.xp_ref.refs_0_, f32[8,128]{1,0:T(8,128)} %maximum_maximum_fusion.par_ref.refs_1_, f32[1024,128]{1,0:T(8,128)} %get-tuple-element.108.colg_ref.refs_2_, f32[1024,128]{1,0:T(8,128)} %copy-done.31, ...), custom_call_target="tpu_custom_call" | custom-call | tf_op jit(solution)/shard_map/gate_bwd/pallas_call | solution.py:135
  593.9 2.4 fusion.7
  596.4 11.8 %pull_first.1.refs_3_ = f32[1024,1024]{1,0:T(8,128)} custom-call(s32[4]{0:T(128)S(1)} %copy-done.39, bf16[1024,3072]{1,0:T(8,128)(2,1)} %get-tuple-element.180.g_ref, bf16[1024,128]{1,0:T(8,128)(2,1)S(1)} %copy-done.17, bf16[256,3200]{1,0:T(8,128)(2,1)S(1)} %copy-done.10, bf16[256,3200]{1,0:T(8,128)(2,1)} %collective-permute-done.refs_5_.refs_1_, ...), custom_call_target="tpu_custom_call" | custom-call | tf_op jit(solution)/shard_map/pull_first/pallas_call | solution.py:599
  610.3 2.4 collective-permute-start.25
  616.2 3.4 collective-permute-done.23
  619.6 10.6 %collective-permute-done.24 = bf16[32,4096]{1,0:T(8,128)(2,1)S(1)} collective-permute-done((bf16[32,4096]{1,0:T(8,128)(2,1)S(1)}, bf16[32,4096]{1,0:T(8,128)(2,1)S(1)}, u32[]{:S(2)}, u32[]{:S(2)}) %collective-permute-start.24) | collective-permute-done | bytes 262176 | tf_op jit(solution)/shard_map/ppermute | solution.py:492
  630.3 4.0 collective-permute-start.28
  636.9 14.4 %pull_second.1 = (bf16[1024,1024]{1,0:T(8,128)(2,1)}, f32[8,1024]{1,0:T(8,128)}) custom-call(bf16[1024,1536]{1,0:T(8,128)(2,1)} %get-tuple-element.186.g_ref.refs_0_, bf16[1024,1536]{1,0:T(8,128)(2,1)} %get-tuple-element.164.g_ref.refs_1_, bf16[1024,4096]{1,0:T(8,128)(2,1)} %all-gather.4.cloned.1.call-done.refs_2_, f32[1024,1024]{1,0:T(8,128)} %pull_first.1.refs_3_, ...), custom_call_target="tpu_custom_call" | custom-call | tf_op jit(solution)/shard_map/pull_second/pallas_call | solution.py:644
  652.1 2.0 collective-permute-start.31
  654.2 2.4 collective-permute-start.33
  659.2 9.0 %collective-permute-done.32 = bf16[32,1536]{1,0:T(8,128)(2,1)S(1)} collective-permute-done((bf16[32,1536]{1,0:T(8,128)(2,1)S(1)}, bf16[32,1536]{1,0:T(8,128)(2,1)S(1)}, u32[]{:S(2)}, u32[]{:S(2)}) %collective-permute-start.32) | collective-permute-done | bytes 98336 | tf_op jit(solution)/shard_map/ppermute | solution.py:492
  671.2 5.0 convert_element_type.266
  681.2 7.0 collective-permute-start.45
  688.2 2.4 collective-permute-start.47
  697.6 2.5 collective-permute-start.43
  700.1 3.3 collective-permute-start.39
  703.5 3.6 collective-permute-done.39
  708.5 2.1 collective-permute-start.49
  710.6 2.3 collective-permute-start.50
  714.4 3.0 collective-permute-done.49
  723.9 6.4 collective-permute-done.20
  735.2 6.5 collective-permute-done.44
  743.0 5.0 collective-permute-done.51
  752.9 3.5 convert_element_type.264
  (339 shorter events, 91.8 us)
Async XLA Ops:
  7.2 124.0 %all-gather.4.cloned.1.call-start = ((), (), s32[]{:S(2)}) async-start(), calls=%async_computation.1 | async-start | bytes 10485760 | tf_op jit(solution)/shard_map/all_gather | solution.py:508
  12.7 73.0 %copy-start.9 = (bf16[256,3200]{1,0:T(8,128)(2,1)}, bf16[256,3200]{1,0:T(8,128)(2,1)S(1)}, u32[]{:S(2)}) copy-start(bf16[256,3200]{1,0:T(8,128)(2,1)S(1)} %get-tuple-element.107.refs_4_.refs_0_) | copy-start | bytes 4915204
  12.7 67.6 %copy-start.69 = (f32[8]{0:T(128)S(1)}, f32[8]{0:T(128)}, u32[]{:S(2)}) copy-start(f32[8]{0:T(128)} %param.23) | copy-start | bytes 100
  12.7 67.6 %copy-start.68 = (f32[8]{0:T(128)S(1)}, f32[8]{0:T(128)}, u32[]{:S(2)}) copy-start(f32[8]{0:T(128)} %param.24) | copy-start | bytes 100
  12.8 71.0 %copy-start.65 = (f32[1024]{0:T(1024)S(1)}, f32[1024]{0:T(1024)}, u32[]{:S(2)}) copy-start(f32[1024]{0:T(1024)} %param.19) | copy-start | bytes 12292
  12.8 166.8 %all-gather.6.cloned.1.call-start = ((), (), s32[]{:S(2)}) async-start(), calls=%async_computation.2 | async-start | bytes 14417920 | tf_op jit(solution)/shard_map/all_gather | solution.py:508
  13.5 209.8 %all-gather.8.cloned.1.call-start = ((), (), s32[]{:S(2)}) async-start(), calls=%async_computation.3 | async-start | bytes 7208960 | tf_op jit(solution)/shard_map/all_gather | solution.py:508
  13.6 65.7 %collective-permute-start.1 = (bf16[256,3200]{1,0:T(8,128)(2,1)S(1)}, bf16[256,3200]{1,0:T(8,128)(2,1)S(1)}, u32[]{:S(2)}, u32[]{:S(2)}) collective-permute-start(bf16[256,3200]{1,0:T(8,128)(2,1)S(1)} %get-tuple-element.107.refs_4_.refs_0_), channel_id=1, source_target_pairs={{0,2},{1,3},{2,0},{3,1},{4,6},{5,7},{6,4},{7,5},{8,10},{9,11},{10,... | collective-permute-start | bytes 4915208 | tf_op jit(solution)/shard_map/ppermute | solution.py:492
  16.6 69.1 %collective-permute-start = (bf16[256,3200]{1,0:T(8,128)(2,1)S(1)}, bf16[256,3200]{1,0:T(8,128)(2,1)}, u32[]{:S(2)}, u32[]{:S(2)}) collective-permute-start(bf16[256,3200]{1,0:T(8,128)(2,1)S(1)} %get-tuple-element.107.refs_4_.refs_0_), channel_id=1, source_target_pairs={{0,1},{1,0},{2,3},{3,2},{4,5},{5,4},{6,7},{7,6},{8,9},{9,8},{10,11... | collective-permute-start | bytes 4915208 | tf_op jit(solution)/shard_map/ppermute | solution.py:492
  79.3 6.4 collective-permute-start.2
  79.3 250.5 %reduce-scatter.2.cloned.1.call-start = ((), (), s32[]{:S(2)}) async-start(), calls=%async_computation.4 | async-start | bytes 7208960 | tf_op jit(solution)/shard_map/reduce_scatter | solution.py:504
  246.0 176.7 %all-reduce.6.cloned.1.call-start = ((), (), s32[]{:S(2)}) async-start(), calls=%async_computation.5 | async-start | bytes 2883584 | tf_op jit(solution)/shard_map/psum | solution.py:806
  292.5 19.2 %collective-permute-start.4 = (bf16[256,5632]{1,0:T(8,128)(2,1)S(1)}, bf16[256,5632]{1,0:T(8,128)(2,1)S(1)}, u32[]{:S(2)}, u32[]{:S(2)}) collective-permute-start(bf16[256,5632]{1,0:T(8,128)(2,1)S(1)} %get-tuple-element.115), channel_id=1, source_target_pairs={{0,1},{1,0},{2,3},{3,2},{4,5},{5,4},{6,7},{7,6},{8,9},{9,8},{10,11... | collective-permute-start | bytes 8650760 | tf_op jit(solution)/shard_map/ppermute | solution.py:492
  292.8 18.9 %collective-permute-start.3 = (bf16[256,5632]{1,0:T(8,128)(2,1)}, bf16[256,5632]{1,0:T(8,128)(2,1)S(1)}, u32[]{:S(2)}, u32[]{:S(2)}) collective-permute-start(bf16[256,5632]{1,0:T(8,128)(2,1)} %get-tuple-element.118), channel_id=1, source_target_pairs={{0,1},{1,0},{2,3},{3,2},{4,5},{5,4},{6,7},{7,6},{8,9},{9,8},{10,11... | collective-permute-start | bytes 8650760 | tf_op jit(solution)/shard_map/ppermute | solution.py:492
  329.6 123.8 %collective-permute-start.9 = (bf16[256,5632]{1,0:T(8,128)(2,1)}, bf16[256,5632]{1,0:T(8,128)(2,1)}, u32[]{:S(2)}, u32[]{:S(2)}) collective-permute-start(bf16[256,5632]{1,0:T(8,128)(2,1)} %get-tuple-element.119), channel_id=1, source_target_pairs={{0,2},{1,3},{2,0},{3,1},{4,6},{5,7},{6,4},{7,5},{8,10},{9,11},{10,... | collective-permute-start | bytes 8650760 | tf_op jit(solution)/shard_map/ppermute | solution.py:492
  334.9 248.7 %all-reduce.8.cloned.1.call-start = ((), (), s32[]{:S(2)}) async-start(), calls=%async_computation.6 | async-start | bytes 5767168 | tf_op jit(solution)/shard_map/psum | solution.py:852
  430.4 10.6 %collective-permute-start.7 = (bf16[256,3072]{1,0:T(8,128)(2,1)S(1)}, bf16[256,3072]{1,0:T(8,128)(2,1)S(1)}, u32[]{:S(2)}, u32[]{:S(2)}) collective-permute-start(bf16[256,3072]{1,0:T(8,128)(2,1)S(1)} %get-tuple-element.138), channel_id=1, source_target_pairs={{0,1},{1,0},{2,3},{3,2},{4,5},{5,4},{6,7},{7,6},{8,9},{9,8},{10,11... | collective-permute-start | bytes 4718600 | tf_op jit(solution)/shard_map/ppermute | solution.py:492
  430.5 10.5 %collective-permute-start.8 = (bf16[256,3072]{1,0:T(8,128)(2,1)S(1)}, bf16[256,3072]{1,0:T(8,128)(2,1)S(1)}, u32[]{:S(2)}, u32[]{:S(2)}) collective-permute-start(bf16[256,3072]{1,0:T(8,128)(2,1)S(1)} %get-tuple-element.133), channel_id=1, source_target_pairs={{0,1},{1,0},{2,3},{3,2},{4,5},{5,4},{6,7},{7,6},{8,9},{9,8},{10,11... | collective-permute-start | bytes 4718600 | tf_op jit(solution)/shard_map/ppermute | solution.py:492
  431.0 5.9 collective-permute-start.5
  431.1 6.6 collective-permute-start.6
  451.9 84.9 %collective-permute-start.12 = (bf16[256,3072]{1,0:T(8,128)(2,1)}, bf16[256,3072]{1,0:T(8,128)(2,1)}, u32[]{:S(2)}, u32[]{:S(2)}) collective-permute-start(bf16[256,3072]{1,0:T(8,128)(2,1)} %get-tuple-element.139), channel_id=1, source_target_pairs={{0,2},{1,3},{2,0},{3,1},{4,6},{5,7},{6,4},{7,5},{8,10},{9,11},{10,... | collective-permute-start | bytes 4718600 | tf_op jit(solution)/shard_map/ppermute | solution.py:492
  459.1 28.5 %copy-start.1 = (bf16[1024,1024]{1,0:T(8,128)(2,1)S(1)}, bf16[1024,1024]{1,0:T(8,128)(2,1)}, u32[]{:S(2)}) copy-start(bf16[1024,1024]{1,0:T(8,128)(2,1)} %fusion.5.refs_0_.refs_1_.refs_2_.refs_3_.a_ref.b_ref) | copy-start | bytes 6291460
  493.2 2.9 collective-permute-start.10
  493.3 3.7 collective-permute-start.11
  493.8 43.0 %collective-permute-start.13 = (bf16[256,1024]{1,0:T(8,128)(2,1)}, bf16[256,1024]{1,0:T(8,128)(2,1)S(1)}, u32[]{:S(2)}, u32[]{:S(2)}) collective-permute-start(bf16[256,1024]{1,0:T(8,128)(2,1)} %copy-done.45), channel_id=1, source_target_pairs={{0,2},{1,3},{2,0},{3,1},{4,6},{5,7},{6,4},{7,5},{8,10},{9,11},{10,... | collective-permute-start | bytes 1572872 | tf_op jit(solution)/shard_map/ppermute | solution.py:492
  496.0 42.5 %copy-start.51 = (bf16[256,4096]{1,0:T(8,128)(2,1)}, bf16[256,4096]{1,0:T(8,128)(2,1)S(1)}, u32[]{:S(2)}) copy-start(bf16[256,4096]{1,0:T(8,128)(2,1)S(1)} %pad_maximum_fusion.1) | copy-start | bytes 6291460
  540.0 51.8 %collective-permute-start.21 = (bf16[128,4096]{1,0:T(8,128)(2,1)}, bf16[128,4096]{1,0:T(8,128)(2,1)}, u32[]{:S(2)}, u32[]{:S(2)}) collective-permute-start(bf16[128,4096]{1,0:T(8,128)(2,1)} %fusion.11), channel_id=1, source_target_pairs={{0,4},{4,0},{8,12},{12,8},{16,20},{20,16},{24,28},{28,24},{1,5},{5... | collective-permute-start | bytes 3145736 | tf_op jit(solution)/shard_map/ppermute | solution.py:492
  541.5 11.6 %collective-permute-start.14 = (bf16[256,1536]{1,0:T(8,128)(2,1)}, bf16[256,1536]{1,0:T(8,128)(2,1)S(1)}, u32[]{:S(2)}, u32[]{:S(2)}) collective-permute-start(bf16[256,1536]{1,0:T(8,128)(2,1)} %get-tuple-element.165), channel_id=1, source_target_pairs={{0,1},{1,0},{2,3},{3,2},{4,5},{5,4},{6,7},{7,6},{8,9},{9,8},{10,11... | collective-permute-start | bytes 2359304 | tf_op jit(solution)/shard_map/ppermute | solution.py:492
  541.5 11.6 %collective-permute-start.15 = (bf16[256,1536]{1,0:T(8,128)(2,1)}, bf16[256,1536]{1,0:T(8,128)(2,1)}, u32[]{:S(2)}, u32[]{:S(2)}) collective-permute-start(bf16[256,1536]{1,0:T(8,128)(2,1)} %get-tuple-element.160), channel_id=1, source_target_pairs={{0,1},{1,0},{2,3},{3,2},{4,5},{5,4},{6,7},{7,6},{8,9},{9,8},{10,11... | collective-permute-start | bytes 2359304 | tf_op jit(solution)/shard_map/ppermute | solution.py:492
  542.0 49.8 %collective-permute-start.22 = (bf16[256,1536]{1,0:T(8,128)(2,1)}, bf16[256,1536]{1,0:T(8,128)(2,1)}, u32[]{:S(2)}, u32[]{:S(2)}) collective-permute-start(bf16[256,1536]{1,0:T(8,128)(2,1)} %get-tuple-element.153), channel_id=1, source_target_pairs={{0,2},{1,3},{2,0},{3,1},{4,6},{5,7},{6,4},{7,5},{8,10},{9,11},{10,... | collective-permute-start | bytes 2359304 | tf_op jit(solution)/shard_map/ppermute | solution.py:492
  559.1 49.1 %collective-permute-start.27 = (bf16[256,1536]{1,0:T(8,128)(2,1)}, bf16[256,1536]{1,0:T(8,128)(2,1)}, u32[]{:S(2)}, u32[]{:S(2)}) collective-permute-start(bf16[256,1536]{1,0:T(8,128)(2,1)} %get-tuple-element.166), channel_id=1, source_target_pairs={{0,2},{1,3},{2,0},{3,1},{4,6},{5,7},{6,4},{7,5},{8,10},{9,11},{10,... | collective-permute-start | bytes 2359304 | tf_op jit(solution)/shard_map/ppermute | solution.py:492
  593.1 42.7 %collective-permute-start.26 = (bf16[128,1536]{1,0:T(8,128)(2,1)S(1)}, bf16[128,1536]{1,0:T(8,128)(2,1)S(1)}, u32[]{:S(2)}, u32[]{:S(2)}) collective-permute-start(bf16[128,1536]{1,0:T(8,128)(2,1)S(1)} %fusion.22), channel_id=1, source_target_pairs={{0,4},{4,0},{8,12},{12,8},{16,20},{20,16},{24,28},{28,24},{1,5},{5... | collective-permute-start | bytes 1179656 | tf_op jit(solution)/shard_map/ppermute | solution.py:492
  608.2 11.3 %collective-permute-start.23 = (bf16[32,4096]{1,0:T(8,128)(2,1)S(1)}, bf16[32,4096]{1,0:T(8,128)(2,1)S(1)}, u32[]{:S(2)}, u32[]{:S(2)}) collective-permute-start(bf16[32,4096]{1,0:T(8,128)(2,1)S(1)} %get-tuple-element.218), channel_id=1, source_target_pairs={{0,8},{4,12},{8,0},{12,4},{16,24},{20,28},{24,16},{28,20},{1,9},{5... | collective-permute-start | bytes 786440 | tf_op jit(solution)/shard_map/ppermute | solution.py:492
  608.8 21.4 %collective-permute-start.24 = (bf16[32,4096]{1,0:T(8,128)(2,1)S(1)}, bf16[32,4096]{1,0:T(8,128)(2,1)S(1)}, u32[]{:S(2)}, u32[]{:S(2)}) collective-permute-start(bf16[32,4096]{1,0:T(8,128)(2,1)S(1)} %get-tuple-element.220), channel_id=1, source_target_pairs={{0,16},{4,20},{8,24},{12,28},{16,0},{20,4},{24,8},{28,12},{1,17},{... | collective-permute-start | bytes 786440 | tf_op jit(solution)/shard_map/ppermute | solution.py:492
  610.3 19.9 %collective-permute-start.25 = (bf16[32,4096]{1,0:T(8,128)(2,1)S(1)}, bf16[32,4096]{1,0:T(8,128)(2,1)S(1)}, u32[]{:S(2)}, u32[]{:S(2)}) collective-permute-start(bf16[32,4096]{1,0:T(8,128)(2,1)S(1)} %get-tuple-element.219), channel_id=1, source_target_pairs={{0,24},{4,28},{8,16},{12,20},{16,8},{20,12},{24,0},{28,4},{1,25},{... | collective-permute-start | bytes 786440 | tf_op jit(solution)/shard_map/ppermute | solution.py:492
  614.5 37.6 %collective-permute-start.34 = (bf16[128,1536]{1,0:T(8,128)(2,1)}, bf16[128,1536]{1,0:T(8,128)(2,1)S(1)}, u32[]{:S(2)}, u32[]{:S(2)}) collective-permute-start(bf16[128,1536]{1,0:T(8,128)(2,1)} %fusion.23), channel_id=1, source_target_pairs={{0,4},{4,0},{8,12},{12,8},{16,20},{20,16},{24,28},{28,24},{1,5},{5... | collective-permute-start | bytes 1179656 | tf_op jit(solution)/shard_map/ppermute | solution.py:492
  630.3 37.9 %collective-permute-start.28 = (bf16[32,4096]{1,0:T(8,128)(2,1)S(1)}, bf16[32,4096]{1,0:T(8,128)(2,1)}, u32[]{:S(2)}, u32[]{:S(2)}) collective-permute-start(bf16[32,4096]{1,0:T(8,128)(2,1)S(1)} %fusion.21), channel_id=1, source_target_pairs={{0,8},{4,12},{8,0},{12,4},{16,24},{20,28},{24,16},{28,20},{1,9},{5... | collective-permute-start | bytes 786440 | tf_op jit(solution)/shard_map/ppermute | solution.py:492
  634.4 33.9 %collective-permute-start.29 = (bf16[32,4096]{1,0:T(8,128)(2,1)S(1)}, bf16[32,4096]{1,0:T(8,128)(2,1)}, u32[]{:S(2)}, u32[]{:S(2)}) collective-permute-start(bf16[32,4096]{1,0:T(8,128)(2,1)S(1)} %fusion.21), channel_id=1, source_target_pairs={{0,16},{4,20},{8,24},{12,28},{16,0},{20,4},{24,8},{28,12},{1,17},{... | collective-permute-start | bytes 786440 | tf_op jit(solution)/shard_map/ppermute | solution.py:492
  652.1 6.7 collective-permute-start.31
  654.2 14.0 %collective-permute-start.32 = (bf16[32,1536]{1,0:T(8,128)(2,1)S(1)}, bf16[32,1536]{1,0:T(8,128)(2,1)S(1)}, u32[]{:S(2)}, u32[]{:S(2)}) collective-permute-start(bf16[32,1536]{1,0:T(8,128)(2,1)S(1)} %get-tuple-element.242), channel_id=1, source_target_pairs={{0,16},{4,20},{8,24},{12,28},{16,0},{20,4},{24,8},{28,12},{1,17},{... | collective-permute-start | bytes 294920 | tf_op jit(solution)/shard_map/ppermute | solution.py:492
  654.2 14.0 %collective-permute-start.33 = (bf16[32,1536]{1,0:T(8,128)(2,1)S(1)}, bf16[32,1536]{1,0:T(8,128)(2,1)S(1)}, u32[]{:S(2)}, u32[]{:S(2)}) collective-permute-start(bf16[32,1536]{1,0:T(8,128)(2,1)S(1)} %get-tuple-element.241), channel_id=1, source_target_pairs={{0,24},{4,28},{8,16},{12,20},{16,8},{20,12},{24,0},{28,4},{1,25},{... | collective-permute-start | bytes 294920 | tf_op jit(solution)/shard_map/ppermute | solution.py:492
  658.9 9.4 %collective-permute-start.30 = (bf16[32,4096]{1,0:T(8,128)(2,1)S(1)}, bf16[32,4096]{1,0:T(8,128)(2,1)S(1)}, u32[]{:S(2)}, u32[]{:S(2)}) collective-permute-start(bf16[32,4096]{1,0:T(8,128)(2,1)S(1)} %fusion.21), channel_id=1, source_target_pairs={{0,24},{4,28},{8,16},{12,20},{16,8},{20,12},{24,0},{28,4},{1,25},{... | collective-permute-start | bytes 786440 | tf_op jit(solution)/shard_map/ppermute | solution.py:492
  669.8 6.5 collective-permute-start.35
  671.0 6.8 collective-permute-start.16
  676.3 3.6 collective-permute-start.36
  677.8 13.9 %collective-permute-start.17 = (f32[362,128]{1,0:T(8,128)S(1)}, f32[362,128]{1,0:T(8,128)S(1)}, u32[]{:S(2)}, u32[]{:S(2)}) collective-permute-start(f32[362,128]{1,0:T(8,128)S(1)} %bitcast_add_fusion.4), channel_id=1, source_target_pairs={{0,2},{1,3},{2,0},{3,1},{4,6},{5,7},{6,4},{7,5},{8,10},{9,11},{10,... | collective-permute-start | bytes 556040 | tf_op jit(solution)/shard_map/ppermute | solution.py:486
  679.9 10.8 %collective-permute-start.37 = (f32[8,128]{1,0:T(8,128)S(1)}, f32[8,128]{1,0:T(8,128)S(1)}, u32[]{:S(2)}, u32[]{:S(2)}) collective-permute-start(f32[8,128]{1,0:T(8,128)S(1)} %fusion.85), channel_id=1, source_target_pairs={{0,4},{1,5},{2,6},{3,7},{4,0},{5,1},{6,2},{7,3},{8,12},{9,13},{10,... | collective-permute-start | bytes 12296 | tf_op jit(solution)/shard_map/ppermute | solution.py:486
  681.2 11.4 %collective-permute-start.45 = (bf16[32,1536]{1,0:T(8,128)(2,1)S(1)}, bf16[32,1536]{1,0:T(8,128)(2,1)S(1)}, u32[]{:S(2)}, u32[]{:S(2)}) collective-permute-start(bf16[32,1536]{1,0:T(8,128)(2,1)S(1)} %get-tuple-element.231), channel_id=1, source_target_pairs={{0,8},{4,12},{8,0},{12,4},{16,24},{20,28},{24,16},{28,20},{1,9},{5... | collective-permute-start | bytes 294920 | tf_op jit(solution)/shard_map/ppermute | solution.py:492
  688.2 9.4 %collective-permute-start.46 = (bf16[32,1536]{1,0:T(8,128)(2,1)S(1)}, bf16[32,1536]{1,0:T(8,128)(2,1)S(1)}, u32[]{:S(2)}, u32[]{:S(2)}) collective-permute-start(bf16[32,1536]{1,0:T(8,128)(2,1)S(1)} %get-tuple-element.233), channel_id=1, source_target_pairs={{0,16},{4,20},{8,24},{12,28},{16,0},{20,4},{24,8},{28,12},{1,17},{... | collective-permute-start | bytes 294920 | tf_op jit(solution)/shard_map/ppermute | solution.py:492
  688.2 11.9 %collective-permute-start.47 = (bf16[32,1536]{1,0:T(8,128)(2,1)S(1)}, bf16[32,1536]{1,0:T(8,128)(2,1)S(1)}, u32[]{:S(2)}, u32[]{:S(2)}) collective-permute-start(bf16[32,1536]{1,0:T(8,128)(2,1)S(1)} %get-tuple-element.232), channel_id=1, source_target_pairs={{0,24},{4,28},{8,16},{12,20},{16,8},{20,12},{24,0},{28,4},{1,25},{... | collective-permute-start | bytes 294920 | tf_op jit(solution)/shard_map/ppermute | solution.py:492
  690.6 4.6 collective-permute-start.38
  691.7 16.7 %collective-permute-start.18 = (f32[362,128]{1,0:T(8,128)S(1)}, f32[362,128]{1,0:T(8,128)S(1)}, u32[]{:S(2)}, u32[]{:S(2)}) collective-permute-start(f32[362,128]{1,0:T(8,128)S(1)} %fusion.86), channel_id=1, source_target_pairs={{0,4},{1,5},{2,6},{3,7},{4,0},{5,1},{6,2},{7,3},{8,12},{9,13},{10,... | collective-permute-start | bytes 556040 | tf_op jit(solution)/shard_map/ppermute | solution.py:486
  692.6 15.9 %collective-permute-start.41 = (bf16[32,1536]{1,0:T(8,128)(2,1)S(1)}, bf16[32,1536]{1,0:T(8,128)(2,1)S(1)}, u32[]{:S(2)}, u32[]{:S(2)}) collective-permute-start(bf16[32,1536]{1,0:T(8,128)(2,1)S(1)} %fusion.39), channel_id=1, source_target_pairs={{0,8},{4,12},{8,0},{12,4},{16,24},{20,28},{24,16},{28,20},{1,9},{5... | collective-permute-start | bytes 294920 | tf_op jit(solution)/shard_map/ppermute | solution.py:492
  695.3 15.3 %collective-permute-start.42 = (bf16[32,1536]{1,0:T(8,128)(2,1)S(1)}, bf16[32,1536]{1,0:T(8,128)(2,1)S(1)}, u32[]{:S(2)}, u32[]{:S(2)}) collective-permute-start(bf16[32,1536]{1,0:T(8,128)(2,1)S(1)} %fusion.39), channel_id=1, source_target_pairs={{0,16},{4,20},{8,24},{12,28},{16,0},{20,4},{24,8},{28,12},{1,17},{... | collective-permute-start | bytes 294920 | tf_op jit(solution)/shard_map/ppermute | solution.py:492
  697.6 15.3 %collective-permute-start.43 = (bf16[32,1536]{1,0:T(8,128)(2,1)S(1)}, bf16[32,1536]{1,0:T(8,128)(2,1)S(1)}, u32[]{:S(2)}, u32[]{:S(2)}) collective-permute-start(bf16[32,1536]{1,0:T(8,128)(2,1)S(1)} %fusion.39), channel_id=1, source_target_pairs={{0,24},{4,28},{8,16},{12,20},{16,8},{20,12},{24,0},{28,4},{1,25},{... | collective-permute-start | bytes 294920 | tf_op jit(solution)/shard_map/ppermute | solution.py:492
  700.1 6.9 collective-permute-start.39
  707.1 42.2 %collective-permute-start.40 = (bf16[128,4096]{1,0:T(8,128)(2,1)S(1)}, bf16[128,4096]{1,0:T(8,128)(2,1)}, u32[]{:S(2)}, u32[]{:S(2)}) collective-permute-start(bf16[128,4096]{1,0:T(8,128)(2,1)S(1)} %get-tuple-element.213), channel_id=1, source_target_pairs={{0,4},{4,0},{8,12},{12,8},{16,20},{20,16},{24,28},{28,24},{1,5},{5... | collective-permute-start | bytes 3145736 | tf_op jit(solution)/shard_map/ppermute | solution.py:492
  708.4 4.7 collective-permute-start.48
  708.5 9.0 %collective-permute-start.49 = (bf16[32,1536]{1,0:T(8,128)(2,1)S(1)}, bf16[32,1536]{1,0:T(8,128)(2,1)S(1)}, u32[]{:S(2)}, u32[]{:S(2)}) collective-permute-start(bf16[32,1536]{1,0:T(8,128)(2,1)S(1)} %fusion.36), channel_id=1, source_target_pairs={{0,16},{4,20},{8,24},{12,28},{16,0},{20,4},{24,8},{28,12},{1,17},{... | collective-permute-start | bytes 294920 | tf_op jit(solution)/shard_map/ppermute | solution.py:492
  710.6 8.1 %collective-permute-start.50 = (bf16[32,1536]{1,0:T(8,128)(2,1)S(1)}, bf16[32,1536]{1,0:T(8,128)(2,1)S(1)}, u32[]{:S(2)}, u32[]{:S(2)}) collective-permute-start(bf16[32,1536]{1,0:T(8,128)(2,1)S(1)} %fusion.36), channel_id=1, source_target_pairs={{0,24},{4,28},{8,16},{12,20},{16,8},{20,12},{24,0},{28,4},{1,25},{... | collective-permute-start | bytes 294920 | tf_op jit(solution)/shard_map/ppermute | solution.py:492
  712.9 7.6 collective-permute-start.19
  713.1 28.6 %collective-permute-start.44 = (bf16[128,1536]{1,0:T(8,128)(2,1)S(1)}, bf16[128,1536]{1,0:T(8,128)(2,1)}, u32[]{:S(2)}, u32[]{:S(2)}) collective-permute-start(bf16[128,1536]{1,0:T(8,128)(2,1)S(1)} %get-tuple-element.234), channel_id=1, source_target_pairs={{0,4},{4,0},{8,12},{12,8},{16,20},{20,16},{24,28},{28,24},{1,5},{5... | collective-permute-start | bytes 1179656 | tf_op jit(solution)/shard_map/ppermute | solution.py:492
  720.5 9.8 %collective-permute-start.20 = (f32[362,128]{1,0:T(8,128)S(1)}, f32[362,128]{1,0:T(8,128)S(1)}, u32[]{:S(2)}, u32[]{:S(2)}) collective-permute-start(f32[362,128]{1,0:T(8,128)S(1)} %add.249), channel_id=1, source_target_pairs={{0,16},{1,17},{2,18},{3,19},{4,20},{5,21},{6,22},{7,23},{8,24},{9,... | collective-permute-start | bytes 556040 | tf_op jit(solution)/shard_map/ppermute | solution.py:486
  722.7 25.3 %collective-permute-start.51 = (bf16[128,1536]{1,0:T(8,128)(2,1)}, bf16[128,1536]{1,0:T(8,128)(2,1)}, u32[]{:S(2)}, u32[]{:S(2)}) collective-permute-start(bf16[128,1536]{1,0:T(8,128)(2,1)} %get-tuple-element.225), channel_id=1, source_target_pairs={{0,4},{4,0},{8,12},{12,8},{16,20},{20,16},{24,28},{28,24},{1,5},{5... | collective-permute-start | bytes 1179656 | tf_op jit(solution)/shard_map/ppermute | solution.py:492
  (65 other events, 434.4 us)
Sparse Core Ops, SparseCore 0:
  12.9 86.1 all-gather.3
  100.7 77.6 all-gather.5
  179.9 43.3 all-gather.7
  246.1 54.8 reduce-scatter.1
  335.0 87.6 all-reduce.5
  457.7 125.9 all-reduce.7
